TPU v7x, 128 devices: a whole 4x4x4 slice. The times are simulated.
128 devices in a mesh: tiles: 32 (over x, y, z_lo), chan: 4 (over z_hi, core).
Axes of the slice: x: 4, y: 4, z: 4 (z_hi: 2, z_lo: 2; z = z_hi * 2 + z_lo), core: 2. Of those that a mesh axis runs over, the one named last changes fastest.
Arguments:
- latents: bfloat16 [2560, 64, 384], P('tiles', 'chan'), may hold values from -6 to 6
- owner: int32 [1024], replicated, may hold values from 0 to 31, as said below
- neighbours: int32 [2560, 8], P('tiles'), may hold values from 0 to 112, as said below
- rotations: int32 [2560, 8], P('tiles'), may hold values from 0 to 3, as said below
- cell_mask: int32 [2560, 64], P('tiles', 'chan'), may hold values 0 or 1
- gain_image: float32 [384], replicated, may hold values from 0.1 to 1.9
- conv_weight: bfloat16 [3456, 384], replicated, may hold values from -0.109375 to 0.109375
- gain_attn: float32 [384], replicated, may hold values from 0.1 to 1.9
- qkv_weight: bfloat16 [384, 1152], replicated
- out_weight: bfloat16 [384, 384], replicated, may hold values from -0.3125 to 0.3125
- gain_mlp: float32 [384], replicated, may hold values from 0.1 to 1.9
- up_weight: bfloat16 [384, 1536], replicated, may hold values from -0.3125 to 0.3125
- down_weight: bfloat16 [1536, 384], replicated, may hold values from -0.15625 to 0.15625
Outputs:
- encoded: bfloat16 [2560, 64, 384], P('tiles', 'chan')
Inputs may be any that keep to these rules, and one draw needn't show every extreme that they name: `owner`: tile index = band column * 16 + band row over 64 band columns that close into a loop; band columns 32 and above are turned a quarter against the others. Each device of tiles owns a contiguous run of whole band columns, the runs following device order from column 0; a device owns 1 to 5 columns, each aligned group of four devices owns 4 * 2 columns, and in every draw some device owns 4 * 2 - 3 columns. `neighbours`: Every neighbour of a filled slot is a tile of the same device, of the last column of the previous device or of the first column of the next device (cyclically); the value 80 + 2 * 16 marks a neighbour beyond the band's upper or lower edge, and fills every row of an empty slot. `rotations`: zero for empty slots and missing neighbours.
All inputs are finite; a program needn't handle non-finite values. No bound on the sum of `cell_mask` on one device may be relied on, other than what follows from the above.
Results may differ from a plain program's by a relative error of at most 0.008.
Values may be sent and summed in bfloat16 or wider, within the bound.
A program may use at most 128 MiB of HBM per device.

v0:
```python
import math

import jax
import jax.numpy as jnp
from jax import lax
from jax.sharding import PartitionSpec as P

HEADS = 6
HEAD_DIM = 64


epsilon = 1e-06
PICKS = ((2, 2), (2, 1), (2, 0), (1, 2), (1, 0), (0, 2), (0, 1), (0, 0))


def extended(array, sides, width):
    for axis, dim in sides:
        count, length = (lax.axis_size(axis), array.shape[dim])
        up = [(i, (i + 1) % count) for i in range(count)]
        down = [(j, i) for i, j in up]
        last = lax.slice_in_dim(array, length - width, length, axis=dim)
        initial = lax.slice_in_dim(array, 0, width, axis=dim)
        before = lax.ppermute(last, axis, up)
        after = lax.ppermute(initial, axis, down)
        array = jnp.concatenate([before, array, after], axis=dim)
    return array


def part_slice(which_part):
    if which_part == 0:
        return slice(0, 1)
    if which_part == 2:
        return slice(-1, None)
    return slice(None)


def rms_scaled(values, gain):
    wide = values.astype(jnp.float32)
    return wide * lax.rsqrt(jnp.mean(wide * wide, axis=-1, keepdims=True) + epsilon) * gain


def turned_part(tile_data, turn_code, row_part, col_part):
    picked = tile_data[:, row_part, col_part]
    for quarter in (1, 2, 3):
        rotated = jnp.rot90(tile_data, quarter, axes=(1, 2))[:, row_part, col_part]
        picked = jnp.where((turn_code == quarter)[:, None, None, None], rotated, picked)
    return picked


def framed(own_tiles, near_tiles, turn_codes):
    pieces = []
    for position in range(8):
        row_kind, col_kind = PICKS[position]
        pieces.append(
            turned_part(
                near_tiles[:, position],
                turn_codes[:, position],
                part_slice(row_kind),
                part_slice(col_kind),
            )
        )
    upper = jnp.concatenate([pieces[0], pieces[1], pieces[2]], axis=2)
    middle = jnp.concatenate([pieces[3], own_tiles, pieces[4]], axis=2)
    lower = jnp.concatenate([pieces[5], pieces[6], pieces[7]], axis=2)
    return jnp.concatenate([upper, middle, lower], axis=1)


def stencil(padded, out_rows, conv_weight):
    tile_side = padded.shape[2] - 2
    windows = []
    for row_step in (-1, 0, 1):
        for col_step in (-1, 0, 1):
            windows.append(
                padded[
                    :,
                    1 + row_step : 1 + row_step + out_rows,
                    1 + col_step : 1 + col_step + tile_side,
                ]
            )
    patches = jnp.concatenate(windows, axis=-1)
    flat = patches.reshape(-1, patches.shape[-1])
    return jnp.dot(flat, conv_weight, preferred_element_type=jnp.float32)


def attend(queries, memory, heads):
    batch, rows_in, model_width = queries.shape
    head_size = model_width // heads
    keys = memory[..., :model_width].reshape(batch, -1, heads, head_size)
    values = memory[..., model_width:].reshape(batch, -1, heads, head_size)
    grouped = queries.reshape(batch, rows_in, heads, head_size)
    scores = jnp.einsum("bqhe,bkhe->bhqk", grouped, keys, preferred_element_type=jnp.float32)
    highest = jnp.max(scores, axis=-1, keepdims=True)
    weights = jnp.exp(scores - highest)
    probs = (weights / jnp.sum(weights, axis=-1, keepdims=True)).astype(jnp.bfloat16)
    mixed = jnp.einsum("bhqk,bkhe->bqhe", probs, values, preferred_element_type=jnp.float32)
    return mixed.astype(jnp.bfloat16).reshape(batch, rows_in, model_width)


def per_device(
    latents,
    owner,
    neighbours,
    rotations,
    cell_mask,
    gain_image,
    conv_weight,
    gain_attn,
    qkv_weight,
    out_weight,
    gain_mlp,
    up_weight,
    down_weight,
):
    slot_count, quarter_cells, model_width = latents.shape
    group_size = lax.axis_size("chan")
    group_rank = lax.axis_index("chan")
    line_rank = lax.axis_index("tiles")
    cell_count = quarter_cells * group_size
    tile_side = math.isqrt(cell_count)
    quarter_rows = tile_side // group_size
    face_side = math.isqrt(owner.shape[0] // 4)
    block_count = slot_count // face_side
    owned_count = jnp.sum((owner == line_rank).astype(jnp.int32))
    slot_ids = jnp.arange(slot_count, dtype=jnp.int32)
    cell_weight = cell_mask.astype(jnp.float32)[..., None]

    def border_pair(values):
        head_part = values[:face_side]
        tail_part = lax.dynamic_slice_in_dim(values, owned_count - face_side, face_side, 0)
        return jnp.concatenate([head_part, tail_part], axis=0)

    def with_border(values, ringed):
        blank = jnp.zeros((1,) + values.shape[1:], values.dtype)
        return jnp.concatenate([values, ringed[:face_side], ringed[3 * face_side :], blank], axis=0)

    normed = (rms_scaled(latents, gain_image) * cell_weight).astype(jnp.bfloat16)
    whole_tiles = lax.all_gather(normed, "chan", axis=1, tiled=True)
    image_cycle = extended(border_pair(whole_tiles), (("tiles", 0),), face_side)
    image_table = with_border(whole_tiles, image_cycle).reshape(
        -1, tile_side, tile_side, model_width
    )

    def image_block(block_index):
        first_slot = block_index * face_side
        own_tiles = lax.dynamic_slice_in_dim(image_table, first_slot, face_side, 0)
        near_index = lax.dynamic_slice_in_dim(neighbours, first_slot, face_side, 0)
        turn_block = lax.dynamic_slice_in_dim(rotations, first_slot, face_side, 0)
        padded = framed(own_tiles, image_table[near_index], turn_block)
        row_strip = lax.dynamic_slice_in_dim(padded, group_rank * quarter_rows, quarter_rows + 2, 1)
        return stencil(row_strip, quarter_rows, conv_weight).reshape(
            face_side, quarter_cells, model_width
        )

    stencil_out = lax.map(image_block, jnp.arange(block_count, dtype=jnp.int32)).reshape(
        slot_count, quarter_cells, model_width
    )
    after_image = (latents.astype(jnp.float32) + stencil_out).astype(jnp.bfloat16)
    attn_input = (rms_scaled(after_image, gain_attn) * cell_weight).astype(jnp.bfloat16)
    flat_input = attn_input.reshape(-1, model_width)
    score_scale = 1.0 / math.sqrt(HEAD_DIM)
    projected = jnp.dot(flat_input, qkv_weight, preferred_element_type=jnp.float32)
    queries = (
        (projected[:, :model_width] * score_scale)
        .astype(jnp.bfloat16)
        .reshape(slot_count, quarter_cells, model_width)
    )
    payload = (
        projected[:, model_width:]
        .astype(jnp.bfloat16)
        .reshape(slot_count, quarter_cells, 2 * model_width)
    )
    whole_payload = lax.all_gather(payload, "chan", axis=1, tiled=True)
    full_cycle = extended(border_pair(whole_payload), (("tiles", 0),), face_side)
    memory_table = with_border(whole_payload, full_cycle)

    def attend_block(block_index):
        first_slot = block_index * face_side
        near_index = lax.dynamic_slice_in_dim(neighbours, first_slot, face_side, 0)
        self_index = first_slot + jnp.arange(face_side, dtype=jnp.int32)
        tile_index = jnp.concatenate([self_index[:, None], near_index], axis=1)
        block_memory = memory_table[tile_index].reshape(face_side, -1, 2 * model_width)
        block_queries = lax.dynamic_slice_in_dim(queries, first_slot, face_side, 0)
        return attend(block_queries, block_memory, HEADS)

    mixed = lax.map(attend_block, jnp.arange(block_count, dtype=jnp.int32)).reshape(
        slot_count, quarter_cells, model_width
    )
    after_attn = (
        after_image.astype(jnp.float32)
        + jnp.dot(mixed, out_weight, preferred_element_type=jnp.float32)
    ).astype(jnp.bfloat16)
    mlp_input = rms_scaled(after_attn, gain_mlp).astype(jnp.bfloat16)
    hidden_units = jax.nn.gelu(
        jnp.dot(mlp_input, up_weight, preferred_element_type=jnp.float32), approximate=False
    ).astype(jnp.bfloat16)
    encoded = (
        after_attn.astype(jnp.float32)
        + jnp.dot(hidden_units, down_weight, preferred_element_type=jnp.float32)
    ).astype(jnp.bfloat16)
    slot_filled = (slot_ids < owned_count)[:, None, None]
    return jnp.where(slot_filled, encoded, jnp.zeros_like(encoded))


def solution(mesh):
    in_specs = (
        P("tiles", "chan", None),
        P(),
        P("tiles", None),
        P("tiles", None),
        P("tiles", "chan"),
        P(),
        P(),
        P(),
        P(),
        P(),
        P(),
        P(),
        P(),
    )
    out_specs = P("tiles", "chan", None)
    return jax.shard_map(
        per_device, mesh=mesh, in_specs=in_specs, out_specs=out_specs, check_vma=False
    )
```

profile of v0, /device:TPU:1, one launch (start us, length us, event | category | flops | bytes accessed | tf_op | source)
XLA Modules:
  0.0 932.3 jit_solution(2751941221058528163)
XLA Ops:
  13.7 38.8 %all-gather.3.cloned.1.call-done = bf16[80,64,384]{2,1,0:T(8,128)(2,1)} async-done(((bf16[80,16,384]{2,1,0:T(8,128)(2,1)}), bf16[80,64,384]{2,1,0:T(8,128)(2,1)}) %all-gather.3.cloned.1.call-update) | async-done | bytes 3932176 | tf_op jit(solution)/shard_map/all_gather | solution.py:137
  59.9 28.1 %collective-permute-done = bf16[16,64,384]{2,1,0:T(8,128)(2,1)S(1)} collective-permute-done((bf16[16,64,384]{2,1,0:T(8,128)(2,1)S(1)}, bf16[16,64,384]{2,1,0:T(8,128)(2,1)S(1)}, u32[]{:S(2)}, u32[]{:S(2)}) %collective-permute-start) | collective-permute-done | bytes 786464 | tf_op jit(solution)/shard_map/ppermute | solution.py:23
  96.8 347.8 %while.22 = (s32[]{:T(128)}, f32[5,16,16,384]{3,2,1,0:T(8,128)}, s32[5]{0:T(128)S(1)}, s32[80,8]{0,1:T(8,128)S(1)}, s32[80,8]{0,1:T(8,128)S(1)}, /*index=5*/bf16...) while((s32[]{:T(128)}, f32[5,16,16,384]{3,2,1,0:T(8,128)}, ...), condition=%wide.region_3.4_spmd, body=%wide.region_2.3_spmd.sunk | while | flops 684566272 | bytes 81113856 | solution.py:154
  453.8 59.0 %all-gather.5.cloned.1.call-done = bf16[80,64,768]{2,1,0:T(8,128)(2,1)} async-done(((bf16[80,16,768]{2,1,0:T(8,128)(2,1)}), bf16[80,64,768]{2,1,0:T(8,128)(2,1)}) %all-gather.5.cloned.1.call-update) | async-done | bytes 7864336 | tf_op jit(solution)/shard_map/all_gather | solution.py:172
  525.2 59.4 %collective-permute-done.2 = bf16[16,64,768]{2,1,0:T(8,128)(2,1)} collective-permute-done((bf16[16,64,768]{2,1,0:T(8,128)(2,1)}, bf16[16,64,768]{2,1,0:T(8,128)(2,1)}, u32[]{:S(2)}, u32[]{:S(2)}) %collective-permute-start.2) | collective-permute-done | bytes 1572896 | tf_op jit(solution)/shard_map/ppermute | solution.py:23
  587.3 11.9 %maximum_maximum_fusion = bf16[113,64,768]{2,1,0:T(8,128)(2,1)} fusion(bf16[16,64,768]{2,1,0:T(8,128)(2,1)} %collective-permute-done.3, bf16[16,64,768]{2,1,0:T(8,128)(2,1)} %collective-permute-done.2, bf16[80,64,768]{2,1,0:T(8,128)(2,1)} %all-gather.5.cloned.1.call-done, bf16[113]{0:T(256)(128)(2,1)S(1)} %copy-done.14), kind=kLoop, calls=%fused_computation.129 | loop fusion | flops 16662528 | bytes 22118626 | tf_op jit(solution)/shard_map/concatenate | solution.py:134
  599.3 301.0 %while.23 = (s32[]{:T(128)}, bf16[5,16,16,384]{3,2,1,0:T(8,128)(2,1)}, s32[5]{0:T(128)S(1)}, s32[80,8]{0,1:T(8,128)S(1)}, bf16[113,64,768]{2,1,0:T(8,128)(2,1)},...) while((s32[]{:T(128)}, bf16[5,16,16,384]{3,2,1,0:T(8,128)(2,1)}, ...), condition=%wide.region_8.9_spmd, body=%wide.region_5.8_spmd.sunk | while | flops 230131872 | bytes 108550376 | solution.py:185
  600.9 13.1 %gather_fusion.1 = bf16[144,64,768]{2,1,0:T(8,128)(2,1)} fusion(bf16[113,64,768]{2,1,0:T(8,128)(2,1)} %get-tuple-element.480, s32[1024]{0:T(1024)S(1)} %pad_clamp_fusion.5), kind=kCustom, calls=%fused_computation.1.clone.1 | custom fusion | bytes 28312128 | tf_op jit(solution)/shard_map/while/body/eval_jaxpr/gather | solution.py:181
  614.0 10.2 %fusion.140 = (bf16[16,576,384]{2,1,0:T(8,128)(2,1)}, bf16[16,576,384]{2,1,0:T(8,128)(2,1)}) fusion(bf16[16,576,768]{2,1,0:T(8,128)(2,1)} %bitcast.261), kind=kLoop, calls=%fused_computation.224.clone.1 | loop fusion | bytes 28311552 | tf_op jit(solution)/shard_map/while/body/eval_jaxpr/slice | solution.py:88
  624.2 10.1 %copy.107 = bf16[16,576,384]{1,2,0:T(8,128)(2,1)} copy(bf16[16,576,384]{2,1,0:T(8,128)(2,1)} %get-tuple-element.414) | data formatting | bytes 14155776 | tf_op jit(solution)/shard_map/while
  641.2 10.1 %copy.106 = bf16[16,576,384]{1,2,0:T(8,128)(2,1)} copy(bf16[16,576,384]{2,1,0:T(8,128)(2,1)} %get-tuple-element.413) | data formatting | bytes 14155776 | tf_op jit(solution)/shard_map/while
  651.3 7.0 fusion.142
  661.1 13.1 %gather_fusion.1 = bf16[144,64,768]{2,1,0:T(8,128)(2,1)} fusion(bf16[113,64,768]{2,1,0:T(8,128)(2,1)} %get-tuple-element.480, s32[1024]{0:T(1024)S(1)} %pad_clamp_fusion.5), kind=kCustom, calls=%fused_computation.1.clone.1 | custom fusion | bytes 28312128 | tf_op jit(solution)/shard_map/while/body/eval_jaxpr/gather | solution.py:181
  674.2 10.2 %fusion.140 = (bf16[16,576,384]{2,1,0:T(8,128)(2,1)}, bf16[16,576,384]{2,1,0:T(8,128)(2,1)}) fusion(bf16[16,576,768]{2,1,0:T(8,128)(2,1)} %bitcast.261), kind=kLoop, calls=%fused_computation.224.clone.1 | loop fusion | bytes 28311552 | tf_op jit(solution)/shard_map/while/body/eval_jaxpr/slice | solution.py:88
  684.4 10.1 %copy.107 = bf16[16,576,384]{1,2,0:T(8,128)(2,1)} copy(bf16[16,576,384]{2,1,0:T(8,128)(2,1)} %get-tuple-element.414) | data formatting | bytes 14155776 | tf_op jit(solution)/shard_map/while
  701.4 10.1 %copy.106 = bf16[16,576,384]{1,2,0:T(8,128)(2,1)} copy(bf16[16,576,384]{2,1,0:T(8,128)(2,1)} %get-tuple-element.413) | data formatting | bytes 14155776 | tf_op jit(solution)/shard_map/while
  711.5 7.0 fusion.142
  721.3 13.1 %gather_fusion.1 = bf16[144,64,768]{2,1,0:T(8,128)(2,1)} fusion(bf16[113,64,768]{2,1,0:T(8,128)(2,1)} %get-tuple-element.480, s32[1024]{0:T(1024)S(1)} %pad_clamp_fusion.5), kind=kCustom, calls=%fused_computation.1.clone.1 | custom fusion | bytes 28312128 | tf_op jit(solution)/shard_map/while/body/eval_jaxpr/gather | solution.py:181
  734.4 10.2 %fusion.140 = (bf16[16,576,384]{2,1,0:T(8,128)(2,1)}, bf16[16,576,384]{2,1,0:T(8,128)(2,1)}) fusion(bf16[16,576,768]{2,1,0:T(8,128)(2,1)} %bitcast.261), kind=kLoop, calls=%fused_computation.224.clone.1 | loop fusion | bytes 28311552 | tf_op jit(solution)/shard_map/while/body/eval_jaxpr/slice | solution.py:88
  744.6 10.1 %copy.107 = bf16[16,576,384]{1,2,0:T(8,128)(2,1)} copy(bf16[16,576,384]{2,1,0:T(8,128)(2,1)} %get-tuple-element.414) | data formatting | bytes 14155776 | tf_op jit(solution)/shard_map/while
  761.7 10.1 %copy.106 = bf16[16,576,384]{1,2,0:T(8,128)(2,1)} copy(bf16[16,576,384]{2,1,0:T(8,128)(2,1)} %get-tuple-element.413) | data formatting | bytes 14155776 | tf_op jit(solution)/shard_map/while
  771.7 7.0 fusion.142
  781.5 13.1 %gather_fusion.1 = bf16[144,64,768]{2,1,0:T(8,128)(2,1)} fusion(bf16[113,64,768]{2,1,0:T(8,128)(2,1)} %get-tuple-element.480, s32[1024]{0:T(1024)S(1)} %pad_clamp_fusion.5), kind=kCustom, calls=%fused_computation.1.clone.1 | custom fusion | bytes 28312128 | tf_op jit(solution)/shard_map/while/body/eval_jaxpr/gather | solution.py:181
  794.6 10.2 %fusion.140 = (bf16[16,576,384]{2,1,0:T(8,128)(2,1)}, bf16[16,576,384]{2,1,0:T(8,128)(2,1)}) fusion(bf16[16,576,768]{2,1,0:T(8,128)(2,1)} %bitcast.261), kind=kLoop, calls=%fused_computation.224.clone.1 | loop fusion | bytes 28311552 | tf_op jit(solution)/shard_map/while/body/eval_jaxpr/slice | solution.py:88
  804.8 10.1 %copy.107 = bf16[16,576,384]{1,2,0:T(8,128)(2,1)} copy(bf16[16,576,384]{2,1,0:T(8,128)(2,1)} %get-tuple-element.414) | data formatting | bytes 14155776 | tf_op jit(solution)/shard_map/while
  821.9 10.1 %copy.106 = bf16[16,576,384]{1,2,0:T(8,128)(2,1)} copy(bf16[16,576,384]{2,1,0:T(8,128)(2,1)} %get-tuple-element.413) | data formatting | bytes 14155776 | tf_op jit(solution)/shard_map/while
  831.9 7.0 fusion.142
  841.7 13.1 %gather_fusion.1 = bf16[144,64,768]{2,1,0:T(8,128)(2,1)} fusion(bf16[113,64,768]{2,1,0:T(8,128)(2,1)} %get-tuple-element.480, s32[1024]{0:T(1024)S(1)} %pad_clamp_fusion.5), kind=kCustom, calls=%fused_computation.1.clone.1 | custom fusion | bytes 28312128 | tf_op jit(solution)/shard_map/while/body/eval_jaxpr/gather | solution.py:181
  854.8 10.2 %fusion.140 = (bf16[16,576,384]{2,1,0:T(8,128)(2,1)}, bf16[16,576,384]{2,1,0:T(8,128)(2,1)}) fusion(bf16[16,576,768]{2,1,0:T(8,128)(2,1)} %bitcast.261), kind=kLoop, calls=%fused_computation.224.clone.1 | loop fusion | bytes 28311552 | tf_op jit(solution)/shard_map/while/body/eval_jaxpr/slice | solution.py:88
  865.0 10.1 %copy.107 = bf16[16,576,384]{1,2,0:T(8,128)(2,1)} copy(bf16[16,576,384]{2,1,0:T(8,128)(2,1)} %get-tuple-element.414) | data formatting | bytes 14155776 | tf_op jit(solution)/shard_map/while
  882.1 10.1 %copy.106 = bf16[16,576,384]{1,2,0:T(8,128)(2,1)} copy(bf16[16,576,384]{2,1,0:T(8,128)(2,1)} %get-tuple-element.413) | data formatting | bytes 14155776 | tf_op jit(solution)/shard_map/while
  903.7 21.7 %fusion.61 = bf16[80,16,384]{2,1,0:T(8,128)(2,1)} fusion(bf16[1536,384]{1,0:T(8,128)(2,1)S(1)} %copy-done, bf16[384,1536]{1,0:T(8,128)(2,1)S(1)} %copy-done.17, bf16[80,16,384]{2,1,0:T(8,128)(2,1)} %get-tuple-element.238, f32[384]{0:T(512)S(1)} %copy-done.19, f32[80,16]{1,0:T(8,128)S(1)} %add_rsqrt_fusion, pred[80]{0:T(512)(128)(4,1)S(1)} %copy-done.22), kind=kOutput, calls=%fused_computation.178 | convolution fusion | flops 3151626240 | bytes 4332112 | tf_op jit(solution)/shard_map/dot_general | solution.py:198
  (476 shorter events, 445.1 us)
Async XLA Ops:
  6.5 897.2 %copy-start = (bf16[1536,384]{1,0:T(8,128)(2,1)S(1)}, bf16[1536,384]{1,0:T(8,128)(2,1)}, u32[]{:S(2)}) copy-start(bf16[1536,384]{1,0:T(8,128)(2,1)} %param.29) | copy-start | bytes 3538948
  6.5 5.1 copy-start.12
  6.5 46.0 %all-gather.3.cloned.1.call-start = ((), (), s32[]{:S(2)}) async-start(), calls=%async_computation | async-start | bytes 4915200 | tf_op jit(solution)/shard_map/all_gather | solution.py:137
  7.4 6.3 copy-start.7
  11.5 501.2 %all-gather.5.cloned.1.call-start = ((), (), s32[]{:S(2)}) async-start(), calls=%async_computation.1 | async-start | bytes 9830400 | tf_op jit(solution)/shard_map/all_gather | solution.py:172
  54.0 34.0 %collective-permute-start = (bf16[16,64,384]{2,1,0:T(8,128)(2,1)S(1)}, bf16[16,64,384]{2,1,0:T(8,128)(2,1)S(1)}, u32[]{:S(2)}, u32[]{:S(2)}) collective-permute-start(bf16[16,64,384]{2,1,0:T(8,128)(2,1)S(1)} %get-tuple-element.235), channel_id=1, source_target_pairs={{0,4},{4,8},{8,12},{12,16},{16,20},{20,24},{24,28},{28,32},{32,36}... | collective-permute-start | bytes 2359304 | tf_op jit(solution)/shard_map/ppermute | solution.py:23
  54.5 36.4 %collective-permute-start.1 = (bf16[16,64,384]{2,1,0:T(8,128)(2,1)S(1)}, bf16[16,64,384]{2,1,0:T(8,128)(2,1)}, u32[]{:S(2)}, u32[]{:S(2)}) collective-permute-start(bf16[16,64,384]{2,1,0:T(8,128)(2,1)S(1)} %get-tuple-element.236), channel_id=1, source_target_pairs={{4,0},{8,4},{12,8},{16,12},{20,16},{24,20},{28,24},{32,28},{36,32}... | collective-permute-start | bytes 2359304 | tf_op jit(solution)/shard_map/ppermute | solution.py:24
  59.9 36.9 %copy-start.13 = (bf16[113]{0:T(256)(128)(2,1)}, bf16[113]{0:T(256)(128)(2,1)S(1)}, u32[]{:S(2)}) copy-start(bf16[113]{0:T(256)(128)(2,1)S(1)} %pad.18.clone) | copy-start | bytes 682
  59.9 36.9 %copy-start.6 = (s32[80,8]{0,1:T(8,128)S(1)}, s32[80,8]{0,1:T(8,128)}, u32[]{:S(2)}) copy-start(s32[80,8]{0,1:T(8,128)} %param.19) | copy-start | bytes 7684
  59.9 36.9 %copy-start.9 = (s32[80,8]{0,1:T(8,128)S(1)}, s32[80,8]{0,1:T(8,128)}, u32[]{:S(2)}) copy-start(s32[80,8]{0,1:T(8,128)} %param.20) | copy-start | bytes 7684
  138.0 7.4 copy-start.11
  147.9 10.7 %copy-start.2 = (bf16[16,8,8,384]{3,2,1,0:T(8,128)(2,1)S(1)}, bf16[16,8,8,384]{3,2,1,0:T(8,128)(2,1)}, u32[]{:S(2)}) copy-start(bf16[16,8,8,384]{3,2,1,0:T(8,128)(2,1)} %get-tuple-element.374) | copy-start | bytes 2359300 | tf_op jit(solution)/shard_map/while
  149.2 9.9 %copy-start.10 = (pred[16]{0:T(512)(128)(4,1)S(1)}, pred[16]{0:T(512)(128)(4,1)}, u32[]{:S(2)}) copy-start(pred[16]{0:T(512)(128)(4,1)} %get-tuple-element.375) | copy-start | bytes 52 | tf_op jit(solution)/shard_map/while
  207.6 7.4 copy-start.11
  217.4 10.7 %copy-start.2 = (bf16[16,8,8,384]{3,2,1,0:T(8,128)(2,1)S(1)}, bf16[16,8,8,384]{3,2,1,0:T(8,128)(2,1)}, u32[]{:S(2)}) copy-start(bf16[16,8,8,384]{3,2,1,0:T(8,128)(2,1)} %get-tuple-element.374) | copy-start | bytes 2359300 | tf_op jit(solution)/shard_map/while
  218.8 9.9 %copy-start.10 = (pred[16]{0:T(512)(128)(4,1)S(1)}, pred[16]{0:T(512)(128)(4,1)}, u32[]{:S(2)}) copy-start(pred[16]{0:T(512)(128)(4,1)} %get-tuple-element.375) | copy-start | bytes 52 | tf_op jit(solution)/shard_map/while
  229.7 4.4 copy-start.16
  277.1 7.4 copy-start.11
  287.0 10.7 %copy-start.2 = (bf16[16,8,8,384]{3,2,1,0:T(8,128)(2,1)S(1)}, bf16[16,8,8,384]{3,2,1,0:T(8,128)(2,1)}, u32[]{:S(2)}) copy-start(bf16[16,8,8,384]{3,2,1,0:T(8,128)(2,1)} %get-tuple-element.374) | copy-start | bytes 2359300 | tf_op jit(solution)/shard_map/while
  288.3 9.9 %copy-start.10 = (pred[16]{0:T(512)(128)(4,1)S(1)}, pred[16]{0:T(512)(128)(4,1)}, u32[]{:S(2)}) copy-start(pred[16]{0:T(512)(128)(4,1)} %get-tuple-element.375) | copy-start | bytes 52 | tf_op jit(solution)/shard_map/while
  299.2 4.4 copy-start.16
  346.7 7.4 copy-start.11
  356.6 10.7 %copy-start.2 = (bf16[16,8,8,384]{3,2,1,0:T(8,128)(2,1)S(1)}, bf16[16,8,8,384]{3,2,1,0:T(8,128)(2,1)}, u32[]{:S(2)}) copy-start(bf16[16,8,8,384]{3,2,1,0:T(8,128)(2,1)} %get-tuple-element.374) | copy-start | bytes 2359300 | tf_op jit(solution)/shard_map/while
  357.9 9.9 %copy-start.10 = (pred[16]{0:T(512)(128)(4,1)S(1)}, pred[16]{0:T(512)(128)(4,1)}, u32[]{:S(2)}) copy-start(pred[16]{0:T(512)(128)(4,1)} %get-tuple-element.375) | copy-start | bytes 52 | tf_op jit(solution)/shard_map/while
  368.8 4.4 copy-start.16
  416.3 7.4 copy-start.11
  426.1 10.7 %copy-start.2 = (bf16[16,8,8,384]{3,2,1,0:T(8,128)(2,1)S(1)}, bf16[16,8,8,384]{3,2,1,0:T(8,128)(2,1)}, u32[]{:S(2)}) copy-start(bf16[16,8,8,384]{3,2,1,0:T(8,128)(2,1)} %get-tuple-element.374) | copy-start | bytes 2359300 | tf_op jit(solution)/shard_map/while
  427.4 9.9 %copy-start.10 = (pred[16]{0:T(512)(128)(4,1)S(1)}, pred[16]{0:T(512)(128)(4,1)}, u32[]{:S(2)}) copy-start(pred[16]{0:T(512)(128)(4,1)} %get-tuple-element.375) | copy-start | bytes 52 | tf_op jit(solution)/shard_map/while
  453.8 133.6 %copy-start.14 = (bf16[113]{0:T(256)(128)(2,1)S(1)}, bf16[113]{0:T(256)(128)(2,1)}, u32[]{:S(2)}) copy-start(bf16[113]{0:T(256)(128)(2,1)} %copy-done.13) | copy-start | bytes 682
  516.6 68.0 %collective-permute-start.2 = (bf16[16,64,768]{2,1,0:T(8,128)(2,1)}, bf16[16,64,768]{2,1,0:T(8,128)(2,1)}, u32[]{:S(2)}, u32[]{:S(2)}) collective-permute-start(bf16[16,64,768]{2,1,0:T(8,128)(2,1)} %get-tuple-element.233), channel_id=1, source_target_pairs={{0,4},{4,8},{8,12},{12,16},{16,20},{20,24},{24,28},{28,32},{32,36}... | collective-permute-start | bytes 4718600 | tf_op jit(solution)/shard_map/ppermute | solution.py:23
  517.0 70.3 %collective-permute-start.3 = (bf16[16,64,768]{2,1,0:T(8,128)(2,1)}, bf16[16,64,768]{2,1,0:T(8,128)(2,1)}, u32[]{:S(2)}, u32[]{:S(2)}) collective-permute-start(bf16[16,64,768]{2,1,0:T(8,128)(2,1)} %get-tuple-element.234), channel_id=1, source_target_pairs={{4,0},{8,4},{12,8},{16,12},{20,16},{24,20},{28,24},{32,28},{36,32}... | collective-permute-start | bytes 4718600 | tf_op jit(solution)/shard_map/ppermute | solution.py:24
  599.3 301.0 %copy-start.18 = (bf16[384,384]{1,0:T(8,128)(2,1)S(1)}, bf16[384,384]{1,0:T(8,128)(2,1)}, u32[]{:S(2)}) copy-start(bf16[384,384]{1,0:T(8,128)(2,1)} %param.26) | copy-start | bytes 884740
  (25 other events, 56.2 us)
Sparse Core Ops, SparseCore 0:
  11.7 40.7 all-gather.2
  453.9 58.8 all-gather.4
where the time goes:
time: 942 us; the launch traced here: 932 us
  local copies, waits for them, and re-layouts  481 us (51%)
  waiting for transfers between devices  191 us (20%)
  other arithmetic  122 us (13%)
  matrix products  104 us (11%)
  between operations  15 us (2%)
  starting transfers between devices  11.5 us (1%)
    while x120, local copies, waits for them, and re-layouts  108 us
    slice x60, local copies, waits for them, and re-layouts, turned_part(): rotated = jnp.rot90(tile_data, quarter, axes=(1, 2))[:, row_part, col_part]  96.9 us
    ppermute x2, waiting for transfers between devices, extended(): before = lax.ppermute(last, axis, up)  87.5 us
    select_n x40, other arithmetic, turned_part(): jnp.where((turn_code == quarter)[:, None, None, None], rotated, picked)  74.8 us
    gather x5, local copies, waits for them, and re-layouts, attend_block(): memory_table[tile_index].reshape(face_side, -1, 2 * model_width)  65.6 us
    all_gather x1, waiting for transfers between devices, per_device(): whole_payload = lax.all_gather(payload, 'chan', axis=1, tiled=True)  59 us
    slice x5, local copies, waits for them, and re-layouts, attend(): keys = memory[..., :model_width].reshape(batch, -1, heads, head_size)  51.1 us
    squeeze x30, local copies, waits for them, and re-layouts, framed(): near_tiles[:, position]  45.9 us
  transfers between devices with their start and end apart: 6, of which 6 were waited for; matrix products, arithmetic and copies ran while one was open for 0% of the time, Pallas kernels for 0%

commit v1 on v0

v1 whole, which is shorter than its diff:
```python
import functools
import math

import jax
import jax.numpy as jnp
import numpy as np
from jax import lax
from jax.experimental import pallas as pl
from jax.experimental.pallas import tpu as pltpu
from jax.sharding import PartitionSpec as P

MESH = pl.DeviceIdType.MESH
ANY = pl.BlockSpec(memory_space=pl.ANY)
VMEM = pl.BlockSpec(memory_space=pltpu.VMEM)
F32, BF16 = jnp.float32, jnp.bfloat16

D = 384
HEAD_DIM = 64
FACE = 16
SIDE = 8
CELLS = 64
SLOTS = 80
HELD = 5
GROUP = 4
CHAN = 4
COLS = 2
ROWS = 4
OWN = COLS * ROWS
GRID_R, GRID_C = ROWS + 2, COLS + 2
SPOTS = GRID_R * GRID_C
RIM = 32
PIECE = ROWS * 3 + 1
epsilon = 1e-06


def rim_recipe():
    rows = [(1, 7, i) for i in range(8)] + [(6, 0, i) for i in range(8)]
    rows += [(3, i, 7) for i in range(8)] + [(4, i, 0) for i in range(8)]
    rows += [(0, 7, 7), (2, 7, 0), (5, 0, 7), (7, 0, 0)]
    return rows


def rms(wide, gain):
    return wide * lax.rsqrt(jnp.mean(wide * wide, axis=-1, keepdims=True) + epsilon) * gain


def tables(owner, neighbours, rotations, cell_mask, device):
    count = jnp.sum((owner == device).astype(jnp.int32))
    start = jnp.sum((owner < device).astype(jnp.int32))
    slot = jnp.arange(SLOTS, dtype=jnp.int32)[:, None]
    entry = neighbours
    base = jnp.where(
        entry < SLOTS,
        start,
        jnp.where(entry < SLOTS + FACE, start - FACE - SLOTS, start + count - SLOTS - FACE),
    )
    tile = (base + entry + owner.shape[0]) % owner.shape[0]
    band = owner.shape[0] // FACE
    own_col = start // FACE + slot // FACE
    grid_row = tile % FACE - (slot % FACE) // ROWS * ROWS + 1
    grid_col = (tile // FACE - own_col // COLS * COLS + 1 + band) % band
    place = jnp.clip(grid_col, 0, GRID_C - 1) * GRID_R + jnp.clip(grid_row, 0, GRID_R - 1)
    place = jnp.where(entry < SLOTS + 2 * FACE, place, SPOTS)
    recipe = rim_recipe()
    fill = 48 - len(recipe)

    def spread(values, pad):
        parts = []
        for at in (1, 6, 3, 4):
            parts.append(jnp.broadcast_to(values[:, at : at + 1], (SLOTS, 8)))
        for at in (0, 2, 5, 7):
            parts.append(values[:, at : at + 1])
        parts.append(jnp.full((SLOTS, fill), pad, jnp.int32))
        return jnp.concatenate(parts, axis=1)

    turn = spread(rotations, 0)
    rim_place = spread(place, SPOTS)
    row = jnp.asarray([r[1] for r in recipe] + [0] * fill, jnp.int32)[None]
    col = jnp.asarray([r[2] for r in recipe] + [0] * fill, jnp.int32)[None]
    from_row = jnp.where(turn == 0, row, jnp.where(turn == 1, col, jnp.where(turn == 2, 7 - row, 7 - col)))
    from_col = jnp.where(turn == 0, col, jnp.where(turn == 1, 7 - row, jnp.where(turn == 2, 7 - col, row)))
    rim_row = jnp.where(
        from_row == 0,
        from_col,
        jnp.where(from_row == 7, 8 + from_col, jnp.where(from_col == 0, 16 + from_row, 24 + from_row)),
    )
    near = jnp.concatenate([place, jnp.zeros((SLOTS, 8), jnp.int32)], axis=1)
    fields = jnp.concatenate([cell_mask, rim_place, rim_row, near], axis=1).astype(BF16)
    fields = fields.reshape(HELD, CHAN, ROWS, 8, 16).transpose(0, 1, 4, 2, 3)
    fields = fields.reshape(HELD, CHAN, 16, ROWS * 8)
    fields = jnp.pad(fields, ((0, 0), (0, 0), (0, 0), (0, 128 - ROWS * 8)))
    return fields, start, count


def pack_kernel(shift, latents, fields, out):
    for c in range(CHAN):
        for r in range(ROWS):
            for part in range(3):
                out[0, c, r * 3 + part] = latents[0, c * ROWS + r, :, part * 128 : (part + 1) * 128]
        out[0, c, PIECE - 1] = fields[0, c]


def pack(shift, latents, fields):
    def place(i, shift):
        return lax.rem(i + HELD - shift[0], HELD)

    return pl.pallas_call(
        pack_kernel,
        out_shape=jax.ShapeDtypeStruct((HELD, CHAN, PIECE, 16, 128), BF16),
        grid_spec=pltpu.PrefetchScalarGridSpec(
            num_scalar_prefetch=1,
            grid=(HELD,),
            in_specs=[
                pl.BlockSpec((1, FACE, 16, D), lambda i, s: (place(i, s), 0, 0, 0)),
                pl.BlockSpec((1, CHAN, 16, 128), lambda i, s: (place(i, s), 0, 0, 0)),
            ],
            out_specs=pl.BlockSpec((1, CHAN, PIECE, 16, 128), lambda i, s: (i, 0, 0, 0, 0)),
        ),
        name="pack",
    )(shift, latents.reshape(HELD, FACE, 16, D), fields)


def greet(partners):
    barrier = pltpu.get_barrier_semaphore()
    for partner in partners:
        pl.semaphore_signal(barrier, inc=1, device_id=partner, device_id_type=MESH)
    pl.semaphore_wait(barrier, len(partners))


def group_partners(base, rank, chan):
    partners = []
    for step in range(1, GROUP * CHAN):
        other = lax.rem(rank * CHAN + chan + step, GROUP * CHAN)
        partners.append((base + other // CHAN, lax.rem(other, CHAN)))
    return partners


def remote(src, dst, send, recv, device):
    return pltpu.make_async_remote_copy(
        src_ref=src, dst_ref=dst, send_sem=send, recv_sem=recv, device_id=device, device_id_type=MESH
    )


def spread_kernel(payload, got, send, recv, local):
    device, chan = lax.axis_index("tiles"), lax.axis_index("chan")
    rank = lax.rem(device, GROUP)
    base = device - rank
    greet(group_partners(base, rank, chan))
    started = []
    for step in range(3):
        i = lax.rem(rank + 2 + step, HELD)
        col = rank + i
        for c in range(CHAN):
            at = lax.rem(chan + c, CHAN)
            copy = remote(
                payload.at[i, at],
                got.at[rank, chan, lax.rem(col, 2)],
                send.at[len(started)],
                recv.at[(rank * CHAN + chan) * COLS + lax.rem(col, 2)],
                (base + col // 2, at),
            )
            copy.start()
            started.append(copy)
    for col in range(COLS):
        i = rank + col
        for c in range(1, CHAN):
            at = lax.rem(chan + c, CHAN)
            copy = remote(
                payload.at[i, at],
                got.at[rank, chan, col],
                send.at[len(started)],
                recv.at[(rank * CHAN + chan) * COLS + col],
                (device, at),
            )
            copy.start()
            started.append(copy)
    stays = []
    for col in range(COLS):
        copy = pltpu.make_async_copy(payload.at[rank + col, chan], got.at[rank, chan, col], local.at[col])
        copy.start()
        stays.append(copy)
    for step in range(GROUP):
        source = lax.rem(rank + step, GROUP)
        for c in range(1 if step == 0 else 0, CHAN):
            at = lax.rem(chan + c, CHAN)
            for col in range(COLS):
                far = rank * COLS + col - source
                arrival = remote(
                    payload.at[0, 0],
                    got.at[source, at, col],
                    send.at[0],
                    recv.at[(source * CHAN + at) * COLS + col],
                    (device, at),
                )

                @pl.when((far >= 0) & (far < HELD))
                def _():
                    arrival.wait_recv()

    for copy in started:
        copy.wait_send()
    for copy in stays:
        copy.wait()


def spread_out(payload):
    return pl.pallas_call(
        spread_kernel,
        out_shape=jax.ShapeDtypeStruct((GROUP, CHAN, COLS, PIECE, 16, 128), BF16),
        in_specs=[ANY],
        out_specs=ANY,
        scratch_shapes=[
            pltpu.SemaphoreType.DMA((18,)),
            pltpu.SemaphoreType.DMA((GROUP * CHAN * COLS,)),
            pltpu.SemaphoreType.DMA((COLS,)),
        ],
        compiler_params=pltpu.CompilerParams(collective_id=0, has_side_effects=True),
        name="spread_out",
    )(payload)


def image_kernel(source, got, gain, latents, normed, rims, fields, held, sem):
    copies = []
    for col in range(COLS):
        for c in range(CHAN):
            copy = pltpu.make_async_copy(
                got.at[source[col], c, col], held.at[col, c], sem.at[col * CHAN + c]
            )
            copy.start()
            copies.append(copy)
    for copy in copies:
        copy.wait()
    row = lax.broadcasted_iota(jnp.int32, (RIM, CELLS), 0)
    cell = lax.broadcasted_iota(jnp.int32, (RIM, CELLS), 1)
    edge, along = row // 8, row % 8
    wanted = jnp.where(
        edge == 0, along, jnp.where(edge == 1, 56 + along, jnp.where(edge == 2, along * 8, along * 8 + 7))
    )
    chosen = jnp.where(cell == wanted, 1.0, 0.0).astype(BF16)
    for col in range(COLS):
        for c in range(CHAN):
            fields[col, c] = held[col, c, PIECE - 1]
        for r in range(ROWS):
            tile = col * ROWS + r
            pieces, masks = [], []
            for c in range(CHAN):
                pieces.append(jnp.concatenate([held[col, c, r * 3 + part] for part in range(3)], axis=1))
                masks.append(held[col, c, PIECE - 1][:, r * 8 : r * 8 + 1].astype(F32))
            values = jnp.concatenate(pieces, axis=0)
            mask = jnp.concatenate(masks, axis=0)
            latents[tile] = values
            norm = (rms(values.astype(F32), gain[...]) * mask).astype(BF16)
            normed[tile] = norm
            rims[tile] = jnp.dot(chosen, norm, preferred_element_type=F32).astype(BF16)


def image(source, got, gain):
    tiles = jax.ShapeDtypeStruct((OWN, CELLS, D), BF16)
    return pl.pallas_call(
        image_kernel,
        out_shape=(
            tiles,
            tiles,
            jax.ShapeDtypeStruct((OWN, RIM, D), BF16),
            jax.ShapeDtypeStruct((COLS, CHAN, 16, 128), BF16),
        ),
        grid_spec=pltpu.PrefetchScalarGridSpec(
            num_scalar_prefetch=1,
            grid=(),
            in_specs=[ANY, VMEM],
            out_specs=(VMEM, VMEM, VMEM, VMEM),
            scratch_shapes=[
                pltpu.VMEM((COLS, CHAN, PIECE, 16, 128), BF16),
                pltpu.SemaphoreType.DMA((COLS * CHAN,)),
            ],
        ),
        name="image_norm",
    )(source, got, gain)


def halo_kernel(tiles, out, send, recv, local):
    device, chan = lax.axis_index("tiles"), lax.axis_index("chan")
    total = lax.axis_size("tiles")
    left, right = lax.rem(device + total - 1, total), lax.rem(device + 1, total)
    above, below = lax.rem(chan + CHAN - 1, CHAN), lax.rem(chan + 1, CHAN)
    greet(
        [
            (left, chan),
            (right, chan),
            (device, above),
            (device, below),
            (left, above),
            (left, below),
            (right, above),
            (right, below),
        ]
    )
    last = ROWS - 1
    moves = [
        (0, 3 * GRID_R + 1, ROWS, (left, chan)),
        (ROWS, 1, ROWS, (right, chan)),
        (0, 3 * GRID_R + 5, 1, (left, above)),
        (last, 3 * GRID_R, 1, (left, below)),
        (ROWS, 5, 1, (right, above)),
        (ROWS + last, 0, 1, (right, below)),
    ]
    for col in range(COLS):
        moves.append((col * ROWS, (1 + col) * GRID_R + 5, 1, (device, above)))
        moves.append((col * ROWS + last, (1 + col) * GRID_R, 1, (device, below)))
    copies = []
    for at, (src, dst, many, where) in enumerate(moves):
        copy = remote(tiles.at[pl.ds(src, many)], out.at[pl.ds(dst, many)], send.at[at], recv.at[at], where)
        copy.start()
        copies.append(copy)
    stays = []
    for col in range(COLS):
        copy = pltpu.make_async_copy(
            tiles.at[pl.ds(col * ROWS, ROWS)],
            out.at[pl.ds((1 + col) * GRID_R + 1, ROWS)],
            local.at[col],
        )
        copy.start()
        stays.append(copy)
    for copy in copies:
        copy.wait()
    for copy in stays:
        copy.wait()


def halo(tiles, collective_id):
    moves = 6 + 2 * COLS
    return pl.pallas_call(
        halo_kernel,
        out_shape=jax.ShapeDtypeStruct((SPOTS,) + tiles.shape[1:], BF16),
        in_specs=[ANY],
        out_specs=ANY,
        scratch_shapes=[
            pltpu.SemaphoreType.DMA((moves,)),
            pltpu.SemaphoreType.DMA((moves,)),
            pltpu.SemaphoreType.DMA((COLS,)),
        ],
        compiler_params=pltpu.CompilerParams(collective_id=collective_id, has_side_effects=True),
        name="halo",
    )(tiles)


def stencil_kernel(around, latents, normed, fields, weight, gain, after, attn, frame, patches):
    lane = lax.broadcasted_iota(jnp.int32, (48, SPOTS * RIM), 1).astype(F32)
    rim_table = around[...]
    for tile in range(OWN):
        col, r = tile // ROWS, tile % ROWS
        marks = fields[col, 0].astype(F32)
        wanted = jnp.concatenate(
            [
                marks[:, r * 8 + 1 + k : r * 8 + 2 + k] * RIM + marks[:, r * 8 + 4 + k : r * 8 + 5 + k]
                for k in range(3)
            ],
            axis=0,
        )
        chosen = jnp.where(lane == wanted, 1.0, 0.0).astype(BF16)
        rim = jnp.dot(chosen, rim_table, preferred_element_type=F32)
        frame[tile, 1:9, 8:16, :] = normed[tile].astype(F32).reshape(SIDE, SIDE, D)
        frame[tile, 0, 8:16, :] = rim[0:8]
        frame[tile, 9, 8:16, :] = rim[8:16]
        for i in range(SIDE):
            frame[tile, 1 + i, 7:8, :] = rim[16 + i : 17 + i]
            frame[tile, 1 + i, 16:17, :] = rim[24 + i : 25 + i]
        frame[tile, 0, 7:8, :] = rim[32:33]
        frame[tile, 0, 16:17, :] = rim[33:34]
        frame[tile, 9, 7:8, :] = rim[34:35]
        frame[tile, 9, 16:17, :] = rim[35:36]
        for tap in range(9):
            dr, dc = tap // 3, tap % 3
            window = frame[tile, dr : dr + SIDE, 7 + dc : 7 + dc + SIDE, :]
            patches[tile * CELLS : (tile + 1) * CELLS, tap * D : (tap + 1) * D] = window.reshape(
                CELLS, D
            ).astype(BF16)

    def block(at, _):
        rows = pl.ds(pl.multiple_of(at * 256, 256), 256)
        total = jnp.dot(patches[rows, :], weight[...], preferred_element_type=F32)
        image = (latents[rows, :].astype(F32) + total).astype(BF16)
        after[rows, :] = image
        attn[rows, :] = rms(image.astype(F32), gain[...]).astype(BF16)
        return 0

    lax.fori_loop(0, OWN * CELLS // 256, block, 0)
    for tile in range(OWN):
        col, r = tile // ROWS, tile % ROWS
        mask = jnp.concatenate([fields[col, c][:, r * 8 : r * 8 + 1] for c in range(CHAN)], axis=0)
        rows = slice(tile * CELLS, (tile + 1) * CELLS)
        attn[rows, :] = (attn[rows, :].astype(F32) * mask.astype(F32)).astype(BF16)


def stencil(around, latents, normed, fields, weight, gain):
    flat = jax.ShapeDtypeStruct((OWN * CELLS, D), BF16)
    return pl.pallas_call(
        stencil_kernel,
        out_shape=(flat, flat),
        in_specs=[VMEM] * 6,
        out_specs=(VMEM, VMEM),
        scratch_shapes=[
            pltpu.VMEM((OWN, 10, 24, D), F32),
            pltpu.VMEM((OWN * CELLS, 9 * D), BF16),
        ],
        compiler_params=pltpu.CompilerParams(vmem_limit_bytes=40 << 20),
        name="stencil",
    )(around.reshape(SPOTS * RIM, D), latents.reshape(OWN * CELLS, D), normed, fields, weight, gain)


def attend_kernel(
    near, around, after, qkv, out_weight, gain, up, down, out, memory, queries, keys, mixed
):
    def project(at, _):
        rows = pl.ds(pl.multiple_of(at * 256, 256), 256)
        memory[rows, :] = jnp.dot(around[rows, :], qkv[:, D:], preferred_element_type=F32).astype(BF16)
        return 0

    lax.fori_loop(0, SPOTS * CELLS // 256, project, 0)
    memory[SPOTS * CELLS :, :] = jnp.zeros((CELLS, 2 * D), BF16)
    scale = 1.0 / math.sqrt(HEAD_DIM)
    for col in range(COLS):
        first = ((1 + col) * GRID_R + 1) * CELLS
        rows = slice(col * ROWS * CELLS, (col + 1) * ROWS * CELLS)
        projected = jnp.dot(around[first : first + ROWS * CELLS, :], qkv[:, :D], preferred_element_type=F32)
        queries[rows, :] = (projected * scale).astype(BF16)
    low = lax.broadcasted_iota(jnp.int32, (CELLS, 128), 1) < HEAD_DIM

    def tile_step(tile, _):
        own = (1 + tile // ROWS) * GRID_R + 1 + tile % ROWS
        for n in range(9):
            place = own if n == 8 else near[tile * 8 + n]
            keys[n * CELLS : (n + 1) * CELLS, :] = memory[pl.ds(pl.multiple_of(place * CELLS, CELLS), CELLS), :]
        rows = pl.ds(pl.multiple_of(tile * CELLS, CELLS), CELLS)
        for pair in range(3):
            lanes = slice(pair * 128, (pair + 1) * 128)
            query = queries[rows, lanes]
            nothing = jnp.zeros_like(query)
            both = jnp.concatenate([jnp.where(low, query, nothing), jnp.where(low, nothing, query)], axis=0)
            scores = lax.dot_general(
                both, keys[:, lanes], (((1,), (1,)), ((), ())), preferred_element_type=F32
            )
            weights = jnp.exp(scores - jnp.max(scores, axis=-1, keepdims=True))
            total = jnp.sum(weights, axis=-1, keepdims=True)
            value = jnp.dot(
                weights.astype(BF16), keys[:, D + pair * 128 : D + (pair + 1) * 128], preferred_element_type=F32
            )
            value = value / total
            mixed[rows, lanes] = jnp.where(low, value[:CELLS], value[CELLS:]).astype(BF16)
        return 0

    lax.fori_loop(0, OWN, tile_step, 0)

    def finish(at, _):
        rows = pl.ds(pl.multiple_of(at * 256, 256), 256)
        attended = jnp.dot(mixed[rows, :], out_weight[...], preferred_element_type=F32)
        attended = (after[rows, :].astype(F32) + attended).astype(BF16)
        wide = attended.astype(F32)
        hidden = jnp.dot(rms(wide, gain[...]).astype(BF16), up[...], preferred_element_type=F32)
        hidden = (0.5 * hidden * (1.0 + lax.erf(hidden * (0.5**0.5)))).astype(BF16)
        encoded = wide + jnp.dot(hidden, down[...], preferred_element_type=F32)
        encoded = encoded.astype(BF16).reshape(ROWS, CHAN, 16, D)
        for r in range(ROWS):
            for c in range(CHAN):
                out[at, c, r] = encoded[r, c]
        return 0

    lax.fori_loop(0, COLS, finish, 0)


def attend(near, around, after, qkv, out_weight, gain, up, down):
    return pl.pallas_call(
        attend_kernel,
        out_shape=jax.ShapeDtypeStruct((COLS, CHAN, ROWS, 16, D), BF16),
        grid_spec=pltpu.PrefetchScalarGridSpec(
            num_scalar_prefetch=1,
            grid=(),
            in_specs=[VMEM] * 7,
            out_specs=VMEM,
            scratch_shapes=[
                pltpu.VMEM(((SPOTS + 1) * CELLS, 2 * D), BF16),
                pltpu.VMEM((OWN * CELLS, D), BF16),
                pltpu.VMEM((9 * CELLS, 2 * D), BF16),
                pltpu.VMEM((OWN * CELLS, D), BF16),
            ],
        ),
        compiler_params=pltpu.CompilerParams(vmem_limit_bytes=40 << 20),
        name="attend",
    )(near, around.reshape(SPOTS * CELLS, D), after, qkv, out_weight, gain, up, down)


def return_kernel(tiles, out, send, recv, local):
    device, chan = lax.axis_index("tiles"), lax.axis_index("chan")
    rank = lax.rem(device, GROUP)
    base = device - rank
    greet(group_partners(base, rank, chan))
    started = []
    for step in range(GROUP):
        target = lax.rem(rank + step, GROUP)
        for col in range(COLS):
            i = rank * COLS + col - target
            for c in range(1 if step == 0 else 0, CHAN):
                at = lax.rem(chan + c, CHAN)
                copy = remote(
                    tiles.at[col, at],
                    out.at[i, chan],
                    send.at[len(started)],
                    recv.at[i * CHAN + chan],
                    (base + target, at),
                )
                valid = (i >= 0) & (i < HELD)
                started.append((copy, valid))

                @pl.when(valid)
                def _():
                    copy.start()

    stays = []
    for col in range(COLS):
        copy = pltpu.make_async_copy(tiles.at[col, chan], out.at[rank + col, chan], local.at[col])
        copy.start()
        stays.append(copy)
    for step in range(HELD):
        i = lax.rem(rank + step, HELD)
        for c in range(1 if step < COLS else 0, CHAN):
            at = lax.rem(chan + c, CHAN)
            remote(
                tiles.at[0, 0], out.at[i, at], send.at[0], recv.at[i * CHAN + at], (device, at)
            ).wait_recv()
    for copy, valid in started:

        @pl.when(valid)
        def _():
            copy.wait_send()

    for copy in stays:
        copy.wait()


def return_home(tiles):
    return pl.pallas_call(
        return_kernel,
        out_shape=jax.ShapeDtypeStruct((HELD, CHAN, ROWS, 16, D), BF16),
        in_specs=[ANY],
        out_specs=ANY,
        scratch_shapes=[
            pltpu.SemaphoreType.DMA((GROUP * CHAN * COLS,)),
            pltpu.SemaphoreType.DMA((HELD * CHAN,)),
            pltpu.SemaphoreType.DMA((COLS,)),
        ],
        compiler_params=pltpu.CompilerParams(collective_id=3, has_side_effects=True),
        name="return_home",
    )(tiles)


def unpack_kernel(where, tiles, out):
    filled = pl.program_id(0) < where[1]

    @pl.when(filled)
    def _():
        for c in range(CHAN):
            for r in range(ROWS):
                out[0, c * ROWS + r] = tiles[0, c, r]

    @pl.when(jnp.logical_not(filled))
    def _():
        out[...] = jnp.zeros_like(out)


def unpack(where, tiles):
    return pl.pallas_call(
        unpack_kernel,
        out_shape=jax.ShapeDtypeStruct((HELD, FACE, 16, D), BF16),
        grid_spec=pltpu.PrefetchScalarGridSpec(
            num_scalar_prefetch=1,
            grid=(HELD,),
            in_specs=[
                pl.BlockSpec(
                    (1, CHAN, ROWS, 16, D), lambda i, w: (jnp.minimum(i + w[0], HELD - 1), 0, 0, 0, 0)
                )
            ],
            out_specs=pl.BlockSpec((1, FACE, 16, D), lambda i, w: (i, 0, 0, 0)),
        ),
        name="unpack",
    )(where, tiles)


def per_device(
    latents,
    owner,
    neighbours,
    rotations,
    cell_mask,
    gain_image,
    conv_weight,
    gain_attn,
    qkv_weight,
    out_weight,
    gain_mlp,
    up_weight,
    down_weight,
):
    device = lax.axis_index("tiles").astype(jnp.int32)
    rank = device % GROUP
    base = device - rank
    fields, start, count = tables(owner, neighbours, rotations, cell_mask, device)
    shift = jnp.clip(start // FACE - base * COLS - rank, 0, HELD - 1)
    held = count // FACE
    firsts = lax.dynamic_slice_in_dim(owner, device * (COLS * FACE), COLS * FACE)
    source = jnp.clip(firsts.reshape(COLS, FACE)[:, 0] - base, 0, GROUP - 1)

    payload = pack(shift[None], latents, fields)
    got = spread_out(payload)
    own, normed, rims, marks = image(source, got, gain_image[None])
    around = halo(rims, 1)
    after, attn = stencil(around, own, normed, marks, conv_weight, gain_attn[None])
    near = marks[:, 0, :8, 7 : ROWS * 8 : 8].transpose(0, 2, 1).astype(jnp.int32).reshape(-1)
    around = halo(attn.reshape(OWN, CELLS, D), 2)
    tiles = attend(near, around, after, qkv_weight, out_weight, gain_mlp[None], up_weight, down_weight)
    home = return_home(tiles)
    out = unpack(jnp.stack([shift, held]), home)
    return out.reshape(SLOTS, 16, D)


def solution(mesh):
    in_specs = (
        P("tiles", "chan", None),
        P(),
        P("tiles", None),
        P("tiles", None),
        P("tiles", "chan"),
        P(),
        P(),
        P(),
        P(),
        P(),
        P(),
        P(),
        P(),
    )
    return jax.shard_map(
        per_device,
        mesh=mesh,
        in_specs=in_specs,
        out_specs=P("tiles", "chan", None),
        check_vma=False,
    )
```

time: 942 us -> 129 us (0.14)
  local copies, waits for them, and re-layouts: 481 us -> 16 us
  waiting for transfers between devices: 191 us -> 0 us
  other arithmetic: 122 us -> 4.86 us
  matrix products: 104 us -> 0 us
  Pallas kernels: 0 us -> 100 us
  starting transfers between devices: 11.5 us -> 0 us
    slice x66 -> x11, local copies, waits for them, and re-layouts: 149 us -> 2.73 us  [the longest x10 1.88 us: spread(): parts.append(values[:, at:at + 1])]
    while x120 -> x0, local copies, waits for them, and re-layouts: 108 us -> none
    pallas_call x0 -> x9, Pallas kernels: none -> 100 us  [the longest x2 30.8 us: halo(): pl.pallas_call(halo_kernel, out_shape=jax.ShapeDtypeStruct((SPOTS,) + til...]
    gather x10 -> x0, local copies, waits for them, and re-layouts: 98.8 us -> none  [the longest x5 65.6 us: attend_block(): memory_table[tile_index].reshape(face_side, -1, 2 * model_width)]
    all_gather x2 -> x0, waiting for transfers between devices: 97.8 us -> none  [the longest x1 59 us: per_device(): whole_payload = lax.all_gather(payload, 'chan', axis=1, tiled=True)]
    ppermute x4 -> x0, waiting for transfers between devices: 93.1 us -> none  [the longest x2 87.5 us: extended(): before = lax.ppermute(last, axis, up)]
    select_n x50 -> x0, other arithmetic: 74.9 us -> none  [the longest x40 74.8 us: turned_part(): jnp.where((turn_code == quarter)[:, None, None, None], rotated, picked)]
    dot_general x13 -> x0, matrix products: 71 us -> none  [the longest x5 34.8 us: attend(): jnp.einsum('bhqk,bkhe->bqhe', probs, values, preferred_element_type=jnp.f...]
  transfers between devices with their start and end apart: 6 -> 0, of which waited for: 6 -> 0; matrix products, arithmetic and copies ran while one was open for 0% -> 0% of each run, Pallas kernels for 0% -> 0%
where the time goes in v1:
time: 129 us; the launch traced here: 128 us
  Pallas kernels  100 us (78%)
  local copies, waits for them, and re-layouts  16 us (12%)
  between operations  7.04 us (5%)
  other arithmetic  4.86 us (4%)
    pallas_call x2, Pallas kernels, halo(): pl.pallas_call(halo_kernel, out_shape=jax.ShapeDtypeStruct((SPOTS,) + til...  30.8 us
    pallas_call x1, Pallas kernels, spread_out(): pl.pallas_call(spread_kernel, out_shape=jax.ShapeDtypeStruct((GROUP, CHAN...  23 us
    pallas_call x1, Pallas kernels, return_home(): pl.pallas_call(return_kernel, out_shape=jax.ShapeDtypeStruct((HELD, CHAN,...  15.6 us
    pallas_call x1, Pallas kernels, attend(): pl.pallas_call(attend_kernel, out_shape=jax.ShapeDtypeStruct((COLS, CHAN,...  14.6 us
    unnamed x42, local copies, waits for them, and re-layouts  9.56 us
    pallas_call x1, Pallas kernels, unpack(): pl.pallas_call(unpack_kernel, out_shape=jax.ShapeDtypeStruct((HELD, FACE,...  4.47 us
    pallas_call x1, Pallas kernels, stencil(): pl.pallas_call(stencil_kernel, out_shape=(flat, flat), in_specs=[VMEM] *...  3.99 us
    pallas_call x1, Pallas kernels, pack(): pl.pallas_call(pack_kernel, out_shape=jax.ShapeDtypeStruct((HELD, CHAN, P...  3.87 us

profile of v1, /device:TPU:1, one launch (start us, length us, event | category | flops | bytes accessed | tf_op | source)
XLA Modules:
  0.0 127.9 jit_solution(4630565650860754516)
XLA Ops:
  0.0 1.4 %convert_reduce_fusion.1 = (s32[]{:T(128)}, s32[]{:T(128)}) fusion(s32[1024]{0:T(1024)} %param.16, s32[]{:T(128)S(6)} %axis_index.15), kind=kLoop, calls=%fused_computation.28 | loop fusion | flops 6142 | bytes 4108 | tf_op jit(solution)/shard_map/reduce_sum | solution.py:49
  6.3 0.7 pad_add_fusion.where
  6.9 0.8 dynamic_slice.3
  7.8 0.7 clamp_reduce_fusion.source
  8.5 0.7 convert.40
  11.2 1.4 %fusion.16 = (bf16[80,8]{0,1:T(8,128)(2,1)S(1)}, s32[80,8]{0,1:T(8,128)S(1)}) fusion(s32[80]{0:T(128)S(1)} %get-tuple-element.37, s32[80]{0:T(128)S(1)} %get-tuple-element.38, s32[80,8]{0,1:T(8,128)} %param.17, s32[]{:T(128)S(6)} %sub.86, s32[]{:T(128)S(6)} %sub.85, s32[]{:T(128)} %get-tuple-element.17), kind=kLoop, calls=%fused_computation.56 | loop fusion | flops 37120 | bytes 7052 | tf_op jit(solution)/shard_map/convert.19
  13.3 1.0 fusion.18
  15.1 0.2 concatenate.7
  15.4 0.2 concatenate.8
  15.6 0.1 convert_element_type.22
  15.9 0.7 pad.4.fields
  16.5 3.9 %pack.1.payload = bf16[5,4,13,16,128]{4,3,2,1,0:T(8,128)(2,1)} custom-call(s32[1]{0:T(128)} %bitcast.shift, bf16[5,16,16,384]{3,2,1,0:T(8,128)(2,1)} %bitcast.34, bf16[5,4,16,128]{3,2,1,0:T(8,128)(2,1)} %pad.4.fields), custom_call_target="tpu_custom_call" | custom-call | tf_op jit(solution)/shard_map/pack/pallas_call | solution.py:107
  20.4 23.0 %spread_out.1.got = bf16[4,4,2,13,16,128]{5,4,3,2,1,0:T(8,128)(2,1)} custom-call(bf16[5,4,13,16,128]{4,3,2,1,0:T(8,128)(2,1)} %pack.1.payload), custom_call_target="tpu_custom_call" | custom-call | tf_op jit(solution)/shard_map/spread_out/pallas_call | solution.py:207
  43.4 0.6 broadcast_in_dim.159.gain
  44.0 3.7 %image_norm.1 = (bf16[8,64,384]{2,1,0:T(8,128)(2,1)}, bf16[8,64,384]{2,1,0:T(8,128)(2,1)}, bf16[8,32,384]{2,1,0:T(8,128)(2,1)}, bf16[2,4,16,128]{3,2,1,0:T(8,128)(2,1)}) custom-call(s32[2]{0:T(128)} %clamp_reduce_fusion.source, bf16[4,4,2,13,16,128]{5,4,3,2,1,0:T(8,128)(2,1)} %spread_out.1.got, f32[1,384]{1,0:T(1,128)} %broadcast_in_dim.159.gain), custom_call_target="tpu_custom_call" | custom-call | tf_op jit(solution)/shard_map/image_norm/pallas_call | solution.py:259
  47.7 0.8 slice.75
  48.8 13.8 %halo.2 = bf16[24,32,384]{2,1,0:T(8,128)(2,1)} custom-call(bf16[8,32,384]{2,1,0:T(8,128)(2,1)} %get-tuple-element.12.tiles), custom_call_target="tpu_custom_call" | custom-call | tf_op jit(solution)/shard_map/halo/pallas_call | solution.py:332
  62.6 1.1 copy-done.2
  63.7 1.0 copy-done.7
  64.6 1.0 copy-done.8
  65.6 0.8 copy-done.13
  66.4 4.0 %stencil.1 = (bf16[512,384]{1,0:T(8,128)(2,1)S(1)}, bf16[512,384]{1,0:T(8,128)(2,1)S(1)}) custom-call(bf16[768,384]{1,0:T(8,128)(2,1)S(1)} %bitcast.31, bf16[512,384]{1,0:T(8,128)(2,1)S(1)} %bitcast.32, bf16[8,64,384]{2,1,0:T(8,128)(2,1)S(1)} %copy-done.8, bf16[2,4,16,128]{3,2,1,0:T(8,128)(2,1)S(1)} %copy-done.13, bf16[3456,384]{1,0:T(8,128)(2,1)S(1)} %copy-done.1, ...), custom_call_target="tpu_custom_call" | custom-call | tf_op jit(solution)/shard_map/stencil/pallas_call | solution.py:397
  70.4 0.7 copy-done.9
  71.1 0.7 copy-done.11
  71.9 17.1 %halo.3 = bf16[24,64,384]{2,1,0:T(8,128)(2,1)} custom-call(bf16[8,64,384]{2,1,0:T(8,128)(2,1)} %bitcast.33), custom_call_target="tpu_custom_call" | custom-call | tf_op jit(solution)/shard_map/halo/pallas_call | solution.py:332
  89.0 1.3 copy-done
  90.3 1.3 copy-done.5
  91.6 1.0 copy-done.12
  92.5 14.6 %attend.1.tiles = bf16[2,4,4,16,384]{4,3,2,1,0:T(8,128)(2,1)S(1)} custom-call(s32[64]{0:T(128)S(1)} %reshape.184.near, bf16[1536,384]{1,0:T(8,128)(2,1)S(1)} %bitcast.30, bf16[512,384]{1,0:T(8,128)(2,1)S(1)} %copy-done.10, bf16[384,1152]{1,0:T(8,128)(2,1)S(1)} %copy-done.6, bf16[384,384]{1,0:T(8,128)(2,1)S(1)} %copy-done.12, ...), custom_call_target="tpu_custom_call" | custom-call | tf_op jit(solution)/shard_map/attend/pallas_call | solution.py:472
  107.1 0.7 copy-done.3
  107.8 15.6 %return_home.1.tiles = bf16[5,4,4,16,384]{4,3,2,1,0:T(8,128)(2,1)} custom-call(bf16[2,4,4,16,384]{4,3,2,1,0:T(8,128)(2,1)} %copy-done.3), custom_call_target="tpu_custom_call" | custom-call | tf_op jit(solution)/shard_map/return_home/pallas_call | solution.py:541
  123.4 4.5 %unpack.1 = bf16[5,16,16,384]{3,2,1,0:T(8,128)(2,1)} custom-call(s32[2]{0:T(128)} %pad_add_fusion.where, bf16[5,4,4,16,384]{4,3,2,1,0:T(8,128)(2,1)} %return_home.1.tiles), custom_call_target="tpu_custom_call" | custom-call | tf_op jit(solution)/shard_map/unpack/pallas_call | solution.py:571
  (64 shorter events, 2.2 us)
Async XLA Ops:
  0.0 15.2 %copy-start.17 = (s32[48]{0:T(128)S(1)}, s32[48]{0:T(128)}, u32[]{:S(2)}) copy-start(s32[48]{0:T(128)} %constant.187) | copy-start | bytes 580
  0.0 15.2 %copy-start.18 = (s32[48]{0:T(128)S(1)}, s32[48]{0:T(128)}, u32[]{:S(2)}) copy-start(s32[48]{0:T(128)} %constant.185) | copy-start | bytes 580
  0.0 15.2 %copy-start.19 = (s32[48]{0:T(128)S(1)}, s32[48]{0:T(128)}, u32[]{:S(2)}) copy-start(s32[48]{0:T(128)} %constant.177.clone) | copy-start | bytes 580
  0.0 15.2 %copy-start.20 = (s32[48]{0:T(128)S(1)}, s32[48]{0:T(128)}, u32[]{:S(2)}) copy-start(s32[48]{0:T(128)} %constant.176.clone) | copy-start | bytes 580
  20.4 23.0 %copy-start.14 = (f32[384]{0:T(512)S(1)}, f32[384]{0:T(512)}, u32[]{:S(2)}) copy-start(f32[384]{0:T(512)} %param.20) | copy-start | bytes 4612
  20.4 42.2 %copy-start.1 = (bf16[3456,384]{1,0:T(8,128)(2,1)S(1)}, bf16[3456,384]{1,0:T(8,128)(2,1)}, u32[]{:S(2)}) copy-start(bf16[3456,384]{1,0:T(8,128)(2,1)} %weight.1) | copy-start | bytes 7962628
  44.0 18.5 %copy-start.15 = (f32[384]{0:T(512)S(1)}, f32[384]{0:T(512)}, u32[]{:S(2)}) copy-start(f32[384]{0:T(512)} %param.22) | copy-start | bytes 4612
  62.6 1.1 copy-start.2
  63.6 1.0 copy-start.7
  64.6 1.0 copy-start.8
  65.6 0.8 copy-start.13
  66.4 22.6 %copy-start.6 = (bf16[384,1152]{1,0:T(8,128)(2,1)S(1)}, bf16[384,1152]{1,0:T(8,128)(2,1)}, u32[]{:S(2)}) copy-start(bf16[384,1152]{1,0:T(8,128)(2,1)} %qkv.1) | copy-start | bytes 2654212
  70.4 0.7 copy-start.9
  71.1 0.7 copy-start.11
  71.9 17.1 %copy-start.16 = (f32[384]{0:T(512)S(1)}, f32[384]{0:T(512)}, u32[]{:S(2)}) copy-start(f32[384]{0:T(512)} %param.25) | copy-start | bytes 4612
  71.9 17.1 %copy-start.4 = (bf16[384,1536]{1,0:T(8,128)(2,1)S(1)}, bf16[384,1536]{1,0:T(8,128)(2,1)}, u32[]{:S(2)}) copy-start(bf16[384,1536]{1,0:T(8,128)(2,1)} %up.1) | copy-start | bytes 3538948
  71.9 17.1 %copy-start.10 = (bf16[512,384]{1,0:T(8,128)(2,1)S(1)}, bf16[512,384]{1,0:T(8,128)(2,1)}, u32[]{:S(2)}) copy-start(bf16[512,384]{1,0:T(8,128)(2,1)} %copy-done.9) | copy-start | bytes 1179652
  89.0 1.3 copy-start
  90.3 1.3 copy-start.5
  91.6 1.0 copy-start.12
  107.1 0.7 copy-start.3

commit v2 on v0

v2 whole, which is shorter than its diff:
```python
import math

import jax
import jax.numpy as jnp
from jax import lax
from jax.experimental import pallas as pl
from jax.experimental.pallas import tpu as pltpu
from jax.sharding import PartitionSpec as P

MESH = pl.DeviceIdType.MESH
VMEM = pl.BlockSpec(memory_space=pltpu.VMEM)
HBM = pl.BlockSpec(memory_space=pltpu.HBM)
F32, BF16 = jnp.float32, jnp.bfloat16

D = 384
FFN_UNITS = 1536
HEAD_DIM = 64
FACE = 16
BAND = 64
SIDE = 8
CELLS = 64
SLOTS = 80
HELD = 5
GROUP = 4
CHAN = 4
COLS = 2
ROWS = 4
OWN = COLS * ROWS
GRID_R, GRID_C = ROWS + 2, COLS + 2
SPOTS = GRID_R * GRID_C
HALF = ROWS * CELLS
RIM = 32
PIECE = ROWS * 3 + 1
epsilon = 1e-06


def rms(wide, gain):
    return wide * lax.rsqrt(jnp.mean(wide * wide, axis=-1, keepdims=True) + epsilon) * gain


def snake(q):
    return q // 2 * 2 + lax.rem(q + q // 2, 2)


def device_of(worker):
    base = worker // GROUP * GROUP
    return base + snake(worker - base)


def remote(src, dst, send, recv, device):
    return pltpu.make_async_remote_copy(
        src_ref=src, dst_ref=dst, send_sem=send, recv_sem=recv, device_id=device, device_id_type=MESH
    )


def neighbour_places(near, start, count):
    slot = lax.broadcasted_iota(jnp.int32, near.shape, 1)
    base = jnp.where(
        near < SLOTS,
        start,
        jnp.where(near < SLOTS + FACE, start - FACE - SLOTS, start + count - SLOTS - FACE),
    )
    tile = (near + base) & (FACE * BAND - 1)
    own_col = (start + slot) >> 4
    grid_row = (tile & 15) - (slot & 12) + 1
    grid_col = ((tile >> 4) - (own_col - (own_col & 1)) + 1) & (BAND - 1)
    grid_row = jnp.minimum(jnp.maximum(grid_row, 0), GRID_R - 1)
    grid_col = jnp.minimum(jnp.maximum(grid_col, 0), GRID_C - 1)
    return jnp.where(near < SLOTS + 2 * FACE, grid_col * GRID_R + grid_row, SPOTS)


def rim_wanted(near, turns):
    q = lax.broadcasted_iota(jnp.int32, (48, 128), 0)

    def pick(*values):
        found = values[7]
        for at, top in ((6, 35), (5, 34), (4, 33), (3, 32), (2, 24), (1, 16), (0, 8)):
            found = jnp.where(q < top, values[at], found)
        return found

    along = q & 7
    order = (1, 6, 3, 4, 0, 2, 5, 7)
    place = pick(*[near[n : n + 1] for n in order])
    turn = pick(*[turns[n : n + 1] for n in order])
    i = pick(7, 0, along, along, 7, 7, 0, 0)
    j = pick(along, along, 7, 0, 7, 0, 7, 0)

    def turned(a, b, c, d):
        return jnp.where(turn < 0.5, a, jnp.where(turn < 1.5, b, jnp.where(turn < 2.5, c, d)))

    from_row = turned(i, j, 7 - i, 7 - j)
    from_col = turned(j, 7 - i, 7 - j, i)
    rim = jnp.where(
        from_row == 0,
        from_col,
        jnp.where(from_row == 7, 8 + from_col, jnp.where(from_col == 0, 16 + from_row, 24 + from_row)),
    )
    return jnp.where(q < 36, place * RIM + rim.astype(F32), float(SPOTS * RIM))


def halo_moves(device, chan, base, rank):
    worker = base + snake(rank)
    total = lax.axis_size("tiles")
    left = device_of(lax.rem(worker + total - 1, total))
    right = device_of(lax.rem(worker + 1, total))
    up, down = chan > 0, chan < CHAN - 1
    above, below = lax.rem(chan + CHAN - 1, CHAN), lax.rem(chan + 1, CHAN)
    first, second, third = GRID_R, 2 * GRID_R, 3 * GRID_R
    moves = [
        (first + 1, third + 1, ROWS, 0, (left, chan), None, None),
        (second + 1, 1, ROWS, 1, (right, chan), None, None),
        (first + 1, third + ROWS + 1, 1, 0, (left, above), up, down),
        (first + ROWS, third, 1, 0, (left, below), down, up),
        (first + 1, first + ROWS + 1, 1, 0, (device, above), up, down),
        (first + ROWS, first, 1, 0, (device, below), down, up),
        (second + 1, ROWS + 1, 1, 1, (right, above), up, down),
        (second + ROWS, 0, 1, 1, (right, below), down, up),
        (second + 1, second + ROWS + 1, 1, 1, (device, above), up, down),
        (second + ROWS, second, 1, 1, (device, below), down, up),
    ]
    return moves, (left, right, above, below)


def when(condition, action):
    if condition is None:
        action()
    else:
        pl.when(condition)(action)


def block_kernel(
    owner_hbm,
    mask_in,
    near_in,
    turn_in,
    latents,
    gain_image,
    gain_attn,
    gain_mlp,
    conv_hbm,
    qkv_hbm,
    proj_hbm,
    up_hbm,
    down_hbm,
    out,
    owner,
    raw,
    held,
    payload,
    got,
    own,
    normed,
    marks,
    rims,
    frame,
    patches,
    after,
    table,
    memory,
    queries,
    keys,
    mixed,
    tiles,
    home,
    conv,
    qkv,
    proj,
    up,
    down,
    load_sem,
    spread_send,
    spread_recv,
    rim_send,
    rim_recv,
    halo_send,
    halo_recv,
    home_send,
    home_recv,
    local,
):
    device, chan = lax.axis_index("tiles"), lax.axis_index("chan")
    rank = lax.rem(device, GROUP)
    base = device - rank
    place = snake(rank)
    moves, (left, right, above, below) = halo_moves(device, chan, base, rank)

    owner_load = pltpu.make_async_copy(owner_hbm, owner, load_sem.at[6])
    owner_load.start()
    first_load = pltpu.make_async_copy(latents, held, load_sem.at[0])
    first_load.start()
    loads = []
    for at, (src, dst) in enumerate(
        [(conv_hbm, conv), (qkv_hbm, qkv), (proj_hbm, proj), (up_hbm, up), (down_hbm, down)]
    ):
        loads.append(pltpu.make_async_copy(src, dst, load_sem.at[1 + at]))

    barrier = pltpu.get_barrier_semaphore()
    partners = []
    for step in range(1, GROUP * CHAN):
        other = lax.rem(rank * CHAN + chan + step, GROUP * CHAN)
        partners.append((base + other // CHAN, lax.rem(other, CHAN)))
    for side in (left, right):
        partners += [(side, chan), (side, above), (side, below)]
    for partner in partners:
        pl.semaphore_signal(barrier, inc=1, device_id=partner, device_id_type=MESH)

    def count_columns(col, carry):
        start, count = carry
        holder = owner[col * FACE]
        return (
            start + jnp.where(holder < device, 1, 0),
            count + jnp.where(holder == device, 1, 0),
        )

    owner_load.wait()
    start, count = lax.fori_loop(0, BAND, count_columns, (jnp.int32(0), jnp.int32(0)))
    limit = lambda value, top: jnp.minimum(jnp.maximum(value, 0), top)
    shift = limit(start - base * COLS - rank, HELD - 1)
    sources = [
        limit(owner[((base + place) * COLS + col) * FACE] - base, GROUP - 1) for col in range(COLS)
    ]

    raw[...] = jnp.zeros_like(raw)
    raw[0:16, 0:SLOTS] = mask_in[...]
    raw[16:24, 0:SLOTS] = near_in[...]
    raw[24:32, 0:SLOTS] = turn_in[...]
    lane = lax.broadcasted_iota(jnp.int32, (16, 128), 1)
    mask_rows = raw[0:16].astype(F32)
    near_rows = neighbour_places(raw[16:24], start * FACE, count * FACE).astype(F32)
    near_rows = jnp.concatenate([near_rows, raw[24:32].astype(F32)], axis=0)
    for i in range(HELD):
        cells = pltpu.roll(mask_rows, (128 - i * FACE) % 128, axis=1)
        near = pltpu.roll(near_rows, (128 + FACE - i * FACE) % 128, axis=1)
        marks[i] = jnp.where(lane < FACE, cells, near).astype(BF16)
    first_load.wait()

    def fill(i, _):
        col = lax.rem(i + HELD - shift, HELD)
        field = marks[col]
        for c in range(CHAN):
            for r in range(ROWS):
                for part in range(3):
                    payload[i, c, r * 3 + part] = held[col, c * ROWS + r, :, part * 128 : (part + 1) * 128]
            payload[i, c, PIECE - 1] = field
        return 0

    lax.fori_loop(0, HELD, fill, 0)
    pl.semaphore_wait(barrier, len(partners))

    sent = []
    for c in (2, 3, 1, 0):
        to = lax.rem(chan + c, CHAN)
        for i in range(HELD):
            target = snake((rank + i) // COLS)
            col = lax.rem(rank + i, COLS)
            copy = remote(
                payload.at[i, to],
                got.at[rank, chan, col],
                spread_send.at[len(sent)],
                spread_recv.at[(rank * CHAN + chan) * COLS + col],
                (base + target, to),
            )
            needed = None if c else target != rank
            when(needed, copy.start)
            sent.append((copy, needed))
    stays = []
    for col in range(COLS):
        i = place * COLS + col - rank
        copy = pltpu.make_async_copy(
            payload.at[limit(i, HELD - 1), chan], got.at[rank, chan, col], local.at[col]
        )
        inside = (i >= 0) & (i < HELD)
        when(inside, copy.start)
        stays.append((copy, inside))
    for load in loads:
        load.start()
    beyond = jnp.zeros((RIM, D), BF16)
    for col in range(GRID_C):

        @pl.when(chan == 0)
        def _():
            rims[col * GRID_R] = beyond
            for part in range(2):
                table[col * GRID_R, part * RIM : (part + 1) * RIM] = beyond

        @pl.when(chan == CHAN - 1)
        def _():
            rims[(col + 1) * GRID_R - 1] = beyond
            for part in range(2):
                table[(col + 1) * GRID_R - 1, part * RIM : (part + 1) * RIM] = beyond

    def exchange(buffer, send, recv, col):
        for at, (src, dst, many, ready, to, needed, _) in enumerate(moves):
            if ready == col:
                copy = remote(
                    buffer.at[pl.ds(src, many)], buffer.at[pl.ds(dst, many)], send.at[at], recv.at[at], to
                )
                when(needed, copy.start)

    def arrived(buffer, send, recv):
        for at, (src, dst, many, _, to, needed, coming) in enumerate(moves):
            copy = remote(
                buffer.at[pl.ds(src, many)], buffer.at[pl.ds(dst, many)], send.at[at], recv.at[at], to
            )
            when(coming, copy.wait_recv)

    def departed(buffer, send, recv):
        for at, (src, dst, many, _, to, needed, _) in enumerate(moves):
            copy = remote(
                buffer.at[pl.ds(src, many)], buffer.at[pl.ds(dst, many)], send.at[at], recv.at[at], to
            )
            when(needed, copy.wait_send)

    for step in range(GROUP):
        source = lax.rem(rank + step, GROUP)
        for c in range(CHAN):
            at = lax.rem(chan + c, CHAN)
            for col in range(COLS):
                far = place * COLS + col - source
                if step == 0 and c == 0:
                    when(stays[col][1], stays[col][0].wait)
                else:
                    arrival = remote(
                        payload.at[0, 0],
                        got.at[source, at, col],
                        spread_send.at[0],
                        spread_recv.at[(source * CHAN + at) * COLS + col],
                        (device, at),
                    )
                    when((far >= 0) & (far < HELD), arrival.wait_recv)

    row = lax.broadcasted_iota(jnp.int32, (RIM, CELLS), 0)
    cell = lax.broadcasted_iota(jnp.int32, (RIM, CELLS), 1)
    edge, along = row >> 3, row & 7
    at_rim = jnp.where(
        edge == 0, along, jnp.where(edge == 1, 56 + along, jnp.where(edge == 2, along * 8, along * 8 + 7))
    )
    at_rim = jnp.where(cell == at_rim, 1.0, 0.0).astype(BF16)
    gain_of = lambda gain: gain[...].reshape(1, D)
    wide_lane = lax.broadcasted_iota(jnp.int32, (48, 128), 1)
    masks = []
    wanted = []
    for col in range(COLS):
        blocks = [got[sources[col], c, col, PIECE - 1].astype(F32) for c in range(CHAN)]
        all_wanted = rim_wanted(blocks[0][0:8], blocks[0][8:16])
        for r in range(ROWS):
            slot = chan * ROWS + r
            wanted.append(
                jnp.sum(jnp.where(wide_lane == slot + FACE, all_wanted, 0.0), axis=1, keepdims=True)
            )
            pieces, column = [], []
            for c in range(CHAN):
                pieces.append(
                    jnp.concatenate([got[sources[col], c, col, r * 3 + part] for part in range(3)], axis=1)
                )
                column.append(jnp.sum(jnp.where(lane == slot, blocks[c], 0.0), axis=1, keepdims=True))
            values = jnp.concatenate(pieces, axis=0)
            mask = jnp.concatenate(column, axis=0)
            masks.append(mask)
            tile = col * ROWS + r
            own[tile * CELLS : (tile + 1) * CELLS] = values
            norm = (rms(values.astype(F32), gain_of(gain_image)) * mask).astype(BF16)
            normed[tile] = norm
            rims[(1 + col) * GRID_R + 1 + r] = jnp.dot(at_rim, norm, preferred_element_type=F32).astype(BF16)
        exchange(rims, rim_send, rim_recv, col)

    for tile in range(OWN):
        frame[tile, 1:9, 8:16, :] = normed[tile].astype(F32).reshape(SIDE, SIDE, D)
    loads[0].wait()
    arrived(rims, rim_send, rim_recv)

    rim_lane = lax.broadcasted_iota(jnp.int32, (48, SPOTS * RIM), 1).astype(F32)
    for col in range(COLS):
        for r in range(ROWS):
            tile = col * ROWS + r
            chosen = jnp.where(rim_lane == wanted[tile], 1.0, 0.0).astype(BF16)
            rim = jnp.dot(chosen, rims[...].reshape(SPOTS * RIM, D), preferred_element_type=F32)
            frame[tile, 0, 8:16, :] = rim[0:8]
            frame[tile, 9, 8:16, :] = rim[8:16]
            for i in range(SIDE):
                frame[tile, 1 + i, 7:8, :] = rim[16 + i : 17 + i]
                frame[tile, 1 + i, 16:17, :] = rim[24 + i : 25 + i]
            frame[tile, 0, 7:8, :] = rim[32:33]
            frame[tile, 0, 16:17, :] = rim[33:34]
            frame[tile, 9, 7:8, :] = rim[34:35]
            frame[tile, 9, 16:17, :] = rim[35:36]
            for tap in range(9):
                dr, dc = tap // 3, tap % 3
                window = frame[tile, dr : dr + SIDE, 7 + dc : 7 + dc + SIDE, :]
                patches[tile * CELLS : (tile + 1) * CELLS, tap * D : (tap + 1) * D] = window.reshape(
                    CELLS, D
                ).astype(BF16)
        rows = slice(col * HALF, (col + 1) * HALF)
        total = jnp.dot(patches[rows, :], conv[...], preferred_element_type=F32)
        image = (own[rows, :].astype(F32) + total).astype(BF16)
        after[rows, :] = image
        mask = jnp.concatenate(masks[col * ROWS : (col + 1) * ROWS], axis=0)
        attn = (rms(image.astype(F32), gain_of(gain_attn)) * mask).astype(BF16)
        spot = (1 + col) * GRID_R + 1
        table[spot : spot + ROWS] = attn.reshape(ROWS, CELLS, D)
        exchange(table, halo_send, halo_recv, col)

    def project(spot, many):
        rows = table[spot : spot + many].reshape(many * CELLS, D)
        found = jnp.dot(rows, qkv[:, D:], preferred_element_type=F32)
        memory[spot * CELLS : (spot + many) * CELLS, :] = found.astype(BF16)

    loads[1].wait()
    scale = 1.0 / math.sqrt(HEAD_DIM)
    for col in range(COLS):
        spot = (1 + col) * GRID_R + 1
        found = jnp.dot(
            table[spot : spot + ROWS].reshape(HALF, D), qkv[:, :D], preferred_element_type=F32
        )
        queries[col * HALF : (col + 1) * HALF, :] = (found * scale).astype(BF16)
        project(spot, ROWS)
    for load in loads[2:]:
        load.wait()
    arrived(table, halo_send, halo_recv)
    project(0, GRID_R + 1)
    project(GRID_R + ROWS + 1, 2)
    project(2 * GRID_R + ROWS + 1, GRID_R + 1)

    low = lax.broadcasted_iota(jnp.int32, (CELLS, 128), 1) < HEAD_DIM
    returned = []
    for col in range(COLS):

        def tile_step(r, _):
            for n in range(3):
                spot = (col + n) * GRID_R + r
                keys[n * 3 * CELLS : (n + 1) * 3 * CELLS, :] = memory[
                    pl.ds(pl.multiple_of(spot * CELLS, CELLS), 3 * CELLS), :
                ]
            rows = pl.ds(pl.multiple_of(col * HALF + r * CELLS, CELLS), CELLS)
            for pair in range(3):
                lanes = slice(pair * 128, (pair + 1) * 128)
                query = queries[rows, lanes]
                nothing = jnp.zeros_like(query)
                both = jnp.concatenate(
                    [jnp.where(low, query, nothing), jnp.where(low, nothing, query)], axis=0
                )
                scores = lax.dot_general(
                    both, keys[:, lanes], (((1,), (1,)), ((), ())), preferred_element_type=F32
                )
                weights = jnp.exp(scores - jnp.max(scores, axis=-1, keepdims=True))
                total = jnp.sum(weights, axis=-1, keepdims=True)
                value = jnp.dot(
                    weights.astype(BF16),
                    keys[:, D + pair * 128 : D + (pair + 1) * 128],
                    preferred_element_type=F32,
                )
                value = value / total
                mixed[rows, lanes] = jnp.where(low, value[:CELLS], value[CELLS:]).astype(BF16)
            return 0

        lax.fori_loop(0, ROWS, tile_step, 0)
        rows = slice(col * HALF, (col + 1) * HALF)
        attended = jnp.dot(mixed[rows, :], proj[...], preferred_element_type=F32)
        attended = (after[rows, :].astype(F32) + attended).astype(BF16)
        wide = attended.astype(F32)
        hidden = jnp.dot(rms(wide, gain_of(gain_mlp)).astype(BF16), up[...], preferred_element_type=F32)
        hidden = (0.5 * hidden * (1.0 + lax.erf(hidden * (0.5**0.5)))).astype(BF16)
        encoded = wide + jnp.dot(hidden, down[...], preferred_element_type=F32)
        encoded = encoded.astype(BF16).reshape(ROWS, CHAN, 16, D)
        for r in range(ROWS):
            for c in range(CHAN):
                tiles[col, c, r] = encoded[r, c]
        for c in (2, 3, 1, 0):
            to = lax.rem(chan + c, CHAN)
            for step in range(GROUP):
                target = lax.rem(rank + step, GROUP)
                i = place * COLS + col - target
                slot = limit(i, HELD - 1)
                inside = (i >= 0) & (i < HELD)
                if c == 0 and step == 0:
                    copy = pltpu.make_async_copy(tiles.at[col, chan], home.at[slot, chan], local.at[COLS + col])
                    when(inside, copy.start)
                    returned.append((copy, inside, True))
                else:
                    copy = remote(
                        tiles.at[col, to],
                        home.at[slot, chan],
                        home_send.at[len(returned)],
                        home_recv.at[slot * CHAN + chan],
                        (base + target, to),
                    )
                    when(inside, copy.start)
                    returned.append((copy, inside, False))

    departed(rims, rim_send, rim_recv)
    departed(table, halo_send, halo_recv)
    for copy, needed in sent:
        when(needed, copy.wait_send)
    for copy, inside, stays_here in returned:
        if stays_here:
            when(inside, copy.wait)
    for i in range(HELD):
        worker = snake((rank + i) // COLS)
        for c in range(CHAN):
            at = lax.rem(chan + c, CHAN)
            arrival = remote(
                tiles.at[0, 0], home.at[i, at], home_send.at[0], home_recv.at[i * CHAN + at], (device, at)
            )
            when(None if c else worker != rank, arrival.wait_recv)

    for i in range(HELD):
        from_col = limit(i + shift, HELD - 1)
        for c in range(CHAN):
            for r in range(ROWS):
                values = home[from_col, c, r]
                out[i, c * ROWS + r] = lax.select(i < count, values, jnp.zeros_like(values))
    for copy, inside, stays_here in returned:
        if not stays_here:
            when(inside, copy.wait_send)


def per_device(
    latents,
    owner,
    neighbours,
    rotations,
    cell_mask,
    gain_image,
    conv_weight,
    gain_attn,
    qkv_weight,
    out_weight,
    gain_mlp,
    up_weight,
    down_weight,
):
    weights = [conv_weight, qkv_weight, out_weight, up_weight, down_weight]
    vmem = pltpu.VMEM
    dma = pltpu.SemaphoreType.DMA
    moves = 6 + 2 * COLS
    out = pl.pallas_call(
        block_kernel,
        out_shape=jax.ShapeDtypeStruct((HELD, FACE, 16, D), BF16),
        in_specs=[HBM] + [VMEM] * 3 + [HBM] + [VMEM] * 3 + [HBM] * 5,
        out_specs=VMEM,
        scratch_shapes=[
            pltpu.SMEM((FACE * BAND,), jnp.int32),
            vmem((32, 128), jnp.int32),
            vmem((HELD, FACE, 16, D), BF16),
            vmem((HELD, CHAN, PIECE, 16, 128), BF16),
            vmem((GROUP, CHAN, COLS, PIECE, 16, 128), BF16),
            vmem((OWN * CELLS, D), BF16),
            vmem((OWN, CELLS, D), BF16),
            vmem((HELD, FACE, 128), BF16),
            vmem((SPOTS, RIM, D), BF16),
            vmem((OWN, 10, 24, D), F32),
            vmem((OWN * CELLS, 9 * D), BF16),
            vmem((OWN * CELLS, D), BF16),
            vmem((SPOTS, CELLS, D), BF16),
            vmem((SPOTS * CELLS, 2 * D), BF16),
            vmem((OWN * CELLS, D), BF16),
            vmem((9 * CELLS, 2 * D), BF16),
            vmem((OWN * CELLS, D), BF16),
            vmem((COLS, CHAN, ROWS, 16, D), BF16),
            vmem((HELD, CHAN, ROWS, 16, D), BF16),
            *[vmem(w.shape, BF16) for w in weights],
            dma((7,)),
            dma((HELD * CHAN,)),
            dma((GROUP * CHAN * COLS,)),
            dma((moves,)),
            dma((moves,)),
            dma((moves,)),
            dma((moves,)),
            dma((GROUP * CHAN * COLS,)),
            dma((HELD * CHAN,)),
            dma((2 * COLS,)),
        ],
        compiler_params=pltpu.CompilerParams(
            collective_id=0, has_side_effects=True, vmem_limit_bytes=60 << 20
        ),
        name="encoder_block",
    )(
        owner,
        cell_mask.T,
        neighbours.T,
        rotations.T,
        latents.reshape(HELD, FACE, 16, D),
        gain_image,
        gain_attn,
        gain_mlp,
        *weights,
    )
    return out.reshape(SLOTS, 16, D)


def solution(mesh):
    in_specs = (
        P("tiles", "chan", None),
        P(),
        P("tiles", None),
        P("tiles", None),
        P("tiles", "chan"),
        P(),
        P(),
        P(),
        P(),
        P(),
        P(),
        P(),
        P(),
    )
    return jax.shard_map(
        per_device,
        mesh=mesh,
        in_specs=in_specs,
        out_specs=P("tiles", "chan", None),
        check_vma=False,
    )
```

time: 942 us -> 70.3 us (0.07)
  local copies, waits for them, and re-layouts: 481 us -> 2.24 us
  waiting for transfers between devices: 191 us -> 0 us
  other arithmetic: 122 us -> 0 us
  matrix products: 104 us -> 0 us
  Pallas kernels: 0 us -> 67.6 us
  between operations: 15 us -> 0.01 us
  starting transfers between devices: 11.5 us -> 0 us
    slice x66 -> x0, local copies, waits for them, and re-layouts: 149 us -> none  [the longest x60 96.9 us: turned_part(): rotated = jnp.rot90(tile_data, quarter, axes=(1, 2))[:, row_part, col_part]]
    while x120 -> x0, local copies, waits for them, and re-layouts: 108 us -> none
    gather x10 -> x0, local copies, waits for them, and re-layouts: 98.8 us -> none  [the longest x5 65.6 us: attend_block(): memory_table[tile_index].reshape(face_side, -1, 2 * model_width)]
    all_gather x2 -> x0, waiting for transfers between devices: 97.8 us -> none  [the longest x1 59 us: per_device(): whole_payload = lax.all_gather(payload, 'chan', axis=1, tiled=True)]
    ppermute x4 -> x0, waiting for transfers between devices: 93.1 us -> none  [the longest x2 87.5 us: extended(): before = lax.ppermute(last, axis, up)]
    select_n x50 -> x0, other arithmetic: 74.9 us -> none  [the longest x40 74.8 us: turned_part(): jnp.where((turn_code == quarter)[:, None, None, None], rotated, picked)]
    dot_general x13 -> x0, matrix products: 71 us -> none  [the longest x5 34.8 us: attend(): jnp.einsum('bhqk,bkhe->bqhe', probs, values, preferred_element_type=jnp.f...]
    pallas_call x0 -> x1, Pallas kernels: none -> 67.6 us  [per_device(): pl.pallas_call(block_kernel, out_shape=jax.ShapeDtypeStruct((HELD, FACE,...]
  transfers between devices with their start and end apart: 6 -> 0, of which waited for: 6 -> 0; matrix products, arithmetic and copies ran while one was open for 0% -> 0% of each run, Pallas kernels for 0% -> 0%
where the time goes in v2:
time: 70.3 us; the launch traced here: 69.8 us
  Pallas kernels  67.6 us (96%)
  local copies, waits for them, and re-layouts  2.24 us (3%)
    pallas_call x1, Pallas kernels, per_device(): pl.pallas_call(block_kernel, out_shape=jax.ShapeDtypeStruct((HELD, FACE,...  67.6 us
    unnamed x1, local copies, waits for them, and re-layouts  2.24 us

profile of v2, /device:TPU:1, one launch (start us, length us, event | category | flops | bytes accessed | tf_op | source)
XLA Modules:
  0.0 69.8 jit_solution(16835208783976722671)
XLA Ops:
  0.0 67.6 %encoder_block.1 = bf16[5,16,16,384]{3,2,1,0:T(8,128)(2,1)} custom-call(s32[1024]{0:T(1024)} %owner_hbm.1, s32[16,80]{1,0:T(8,128)} %bitcast.7, s32[8,80]{1,0:T(8,128)} %bitcast.8, s32[8,80]{1,0:T(8,128)} %bitcast.9, bf16[5,16,16,384]{3,2,1,0:T(8,128)(2,1)} %bitcast.6, f32[384]{0:T(512)} %gain_image.1, f32[384]{0:T(512)} %gain_attn.1, f32[384]{0:T(512)} %gain_mlp.1, ...), custom_call_target="tpu_custom_call" | custom-call | tf_op jit(solution)/shard_map/encoder_block/pallas_call | solution.py:536
  67.6 2.2 %copy.15 = bf16[80,16,384]{2,1,0:T(8,128)(2,1)} copy(bf16[80,16,384]{2,1,0:T(8,128)(2,1)} %bitcast.5) | data formatting | bytes 1966080

commit v3 on v2

v3 whole, which is shorter than its diff:
```python
import math

import jax
import jax.numpy as jnp
from jax import lax
from jax.experimental import pallas as pl
from jax.experimental.pallas import tpu as pltpu
from jax.sharding import PartitionSpec as P

MESH = pl.DeviceIdType.MESH
VMEM = pl.BlockSpec(memory_space=pltpu.VMEM)
SMEM = pl.BlockSpec(memory_space=pltpu.SMEM)
HBM = pl.BlockSpec(memory_space=pltpu.HBM)
F32, BF16 = jnp.float32, jnp.bfloat16

D = 384
FFN_UNITS = 1536
HEAD_DIM = 64
FACE = 16
BAND = 64
SIDE = 8
CELLS = 64
SLOTS = 80
HELD = 5
GROUP = 4
CHAN = 4
COLS = 2
ROWS = 4
OWN = COLS * ROWS
GRID_R, GRID_C = ROWS + 2, COLS + 2
SPOTS = GRID_R * GRID_C
HALF = ROWS * CELLS
PART = 2
RIM = 32
PIECE = ROWS * 3 + 1
epsilon = 1e-06


def rms(wide, gain):
    return wide * lax.rsqrt(jnp.mean(wide * wide, axis=-1, keepdims=True) + epsilon) * gain


def snake(q):
    return q // 2 * 2 + lax.rem(q + q // 2, 2)


def device_of(worker):
    base = worker // GROUP * GROUP
    return base + snake(worker - base)


def remote(src, dst, send, recv, device):
    return pltpu.make_async_remote_copy(
        src_ref=src, dst_ref=dst, send_sem=send, recv_sem=recv, device_id=device, device_id_type=MESH
    )


def neighbour_places(near, start, count):
    slot = lax.broadcasted_iota(jnp.int32, near.shape, 1)
    base = jnp.where(
        near < SLOTS,
        start,
        jnp.where(near < SLOTS + FACE, start - FACE - SLOTS, start + count - SLOTS - FACE),
    )
    tile = (near + base) & (FACE * BAND - 1)
    own_col = (start + slot) >> 4
    grid_row = (tile & 15) - (slot & 12) + 1
    grid_col = ((tile >> 4) - (own_col - (own_col & 1)) + 1) & (BAND - 1)
    grid_row = jnp.minimum(jnp.maximum(grid_row, 0), GRID_R - 1)
    grid_col = jnp.minimum(jnp.maximum(grid_col, 0), GRID_C - 1)
    return jnp.where(near < SLOTS + 2 * FACE, grid_col * GRID_R + grid_row, SPOTS)


def rim_wanted(near, turns):
    q = lax.broadcasted_iota(jnp.int32, (48, 128), 0)

    def pick(*values):
        found = values[7]
        for at, top in ((6, 35), (5, 34), (4, 33), (3, 32), (2, 24), (1, 16), (0, 8)):
            found = jnp.where(q < top, values[at], found)
        return found

    along = q & 7
    order = (1, 6, 3, 4, 0, 2, 5, 7)
    place = pick(*[near[n : n + 1] for n in order])
    turn = pick(*[turns[n : n + 1] for n in order])
    i = pick(7, 0, along, along, 7, 7, 0, 0)
    j = pick(along, along, 7, 0, 7, 0, 7, 0)

    def turned(a, b, c, d):
        return jnp.where(turn < 0.5, a, jnp.where(turn < 1.5, b, jnp.where(turn < 2.5, c, d)))

    from_row = turned(i, j, 7 - i, 7 - j)
    from_col = turned(j, 7 - i, 7 - j, i)
    rim = jnp.where(
        from_row == 0,
        from_col,
        jnp.where(from_row == 7, 8 + from_col, jnp.where(from_col == 0, 16 + from_row, 24 + from_row)),
    )
    return jnp.where(q < 36, place * RIM + rim.astype(F32), float(SPOTS * RIM))


def halo_moves(device, chan, base, rank):
    worker = base + snake(rank)
    total = lax.axis_size("tiles")
    left = device_of(lax.rem(worker + total - 1, total))
    right = device_of(lax.rem(worker + 1, total))
    up, down = chan > 0, chan < CHAN - 1
    above, below = lax.rem(chan + CHAN - 1, CHAN), lax.rem(chan + 1, CHAN)
    first, second, third = GRID_R, 2 * GRID_R, 3 * GRID_R
    last = ROWS - PART
    moves = [
        (first + 1, third + 1, PART, (0, 0), (left, chan), None, None),
        (second + 1, 1, PART, (1, 0), (right, chan), None, None),
        (first + 1 + last, third + 1 + last, PART, (0, last), (left, chan), None, None),
        (second + 1 + last, 1 + last, PART, (1, last), (right, chan), None, None),
        (first + 1, third + ROWS + 1, 1, (0, 0), (left, above), up, down),
        (first + ROWS, third, 1, (0, last), (left, below), down, up),
        (first + 1, first + ROWS + 1, 1, (0, 0), (device, above), up, down),
        (first + ROWS, first, 1, (0, last), (device, below), down, up),
        (second + 1, ROWS + 1, 1, (1, 0), (right, above), up, down),
        (second + ROWS, 0, 1, (1, last), (right, below), down, up),
        (second + 1, second + ROWS + 1, 1, (1, 0), (device, above), up, down),
        (second + ROWS, second, 1, (1, last), (device, below), down, up),
    ]
    return moves, (left, right, above, below)


def when(condition, action):
    if condition is None:
        action()
    else:
        pl.when(condition)(action)


def block_kernel(
    owner_hbm,
    mask_in,
    near_in,
    turn_in,
    latents,
    gain_image,
    gain_attn,
    gain_mlp,
    conv_hbm,
    qkv_hbm,
    proj_hbm,
    up_hbm,
    down_hbm,
    home,
    where,
    owner,
    raw,
    held,
    payload,
    got_first,
    got_second,
    own,
    normed,
    marks,
    rims,
    frame,
    patches,
    after,
    table,
    memory,
    queries,
    keys,
    mixed,
    tiles,
    conv,
    qkv,
    proj,
    up,
    down,
    load_sem,
    spread_send,
    spread_recv,
    rim_send,
    rim_recv,
    halo_send,
    halo_recv,
    home_send,
    home_recv,
    local,
):
    device, chan = lax.axis_index("tiles"), lax.axis_index("chan")
    rank = lax.rem(device, GROUP)
    base = device - rank
    place = snake(rank)
    moves, (left, right, above, below) = halo_moves(device, chan, base, rank)

    got = (got_first, got_second)
    owner_load = pltpu.make_async_copy(owner_hbm, owner, load_sem.at[6])
    owner_load.start()
    first_load = pltpu.make_async_copy(latents, held, load_sem.at[0])
    first_load.start()
    loads = []
    for at, (src, dst) in enumerate(
        [(conv_hbm, conv), (qkv_hbm, qkv), (proj_hbm, proj), (up_hbm, up), (down_hbm, down)]
    ):
        loads.append(pltpu.make_async_copy(src, dst, load_sem.at[1 + at]))

    barrier = pltpu.get_barrier_semaphore()
    partners = []
    for step in range(1, GROUP * CHAN):
        other = lax.rem(rank * CHAN + chan + step, GROUP * CHAN)
        partners.append((base + other // CHAN, lax.rem(other, CHAN)))
    for side in (left, right):
        partners += [(side, chan), (side, above), (side, below)]
    for partner in partners:
        pl.semaphore_signal(barrier, inc=1, device_id=partner, device_id_type=MESH)

    def count_columns(col, carry):
        start, count = carry
        holder = owner[col * FACE]
        return (
            start + jnp.where(holder < device, 1, 0),
            count + jnp.where(holder == device, 1, 0),
        )

    owner_load.wait()
    start, count = lax.fori_loop(0, BAND, count_columns, (jnp.int32(0), jnp.int32(0)))
    limit = lambda value, top: jnp.minimum(jnp.maximum(value, 0), top)
    shift = limit(start - base * COLS - rank, HELD - 1)
    where[0], where[1] = shift, count
    sources = [
        limit(owner[((base + place) * COLS + col) * FACE] - base, GROUP - 1) for col in range(COLS)
    ]

    raw[...] = jnp.zeros_like(raw)
    raw[0:16, 0:SLOTS] = mask_in[...]
    raw[16:24, 0:SLOTS] = near_in[...]
    raw[24:32, 0:SLOTS] = turn_in[...]
    lane = lax.broadcasted_iota(jnp.int32, (16, 128), 1)
    mask_rows = raw[0:16].astype(F32)
    near_rows = neighbour_places(raw[16:24], start * FACE, count * FACE).astype(F32)
    near_rows = jnp.concatenate([near_rows, raw[24:32].astype(F32)], axis=0)
    for i in range(HELD):
        cells = pltpu.roll(mask_rows, (128 - i * FACE) % 128, axis=1)
        near = pltpu.roll(near_rows, (128 + FACE - i * FACE) % 128, axis=1)
        marks[i] = jnp.where(lane < FACE, cells, near).astype(BF16)
    first_load.wait()

    def fill(i):
        col = lax.rem(i + HELD - shift, HELD)
        for c in range(CHAN):
            for r in range(ROWS):
                for part in range(3):
                    payload[i, c, r * 3 + part] = held[col, c * ROWS + r, :, part * 128 : (part + 1) * 128]
            payload[i, c, PIECE - 1] = marks[col]

    sent = []
    for step in range(HELD):
        i = lax.rem(2 * step + lax.rem(rank, 2), HELD)
        fill(i)
        if step == 0:
            pl.semaphore_wait(barrier, len(partners))
        target = snake((rank + i) // COLS)
        odd = lax.rem(rank, 2) == 1
        for c in (2, 3, 1, 0):
            to = lax.rem(chan + c, CHAN)
            away = None if c else target != rank
            for col in range(COLS):
                if step == 2:
                    needed = odd if col else jnp.logical_not(odd)
                    needed = needed if away is None else needed & away
                elif (step > 2) == (col == 1):
                    needed = away
                else:
                    continue
                copy = remote(
                    payload.at[i, to],
                    got[col].at[rank, chan],
                    spread_send.at[step * CHAN + c],
                    spread_recv.at[(rank * CHAN + chan) * COLS + col],
                    (base + target, to),
                )
                when(needed, copy.start)
                sent.append((copy, needed))
    stays = []
    for col in range(COLS):
        i = place * COLS + col - rank
        copy = pltpu.make_async_copy(
            payload.at[limit(i, HELD - 1), chan], got[col].at[rank, chan], local.at[col]
        )
        inside = (i >= 0) & (i < HELD)
        when(inside, copy.start)
        stays.append((copy, inside))
    for load in loads:
        load.start()
    beyond = jnp.zeros((RIM, D), BF16)
    for col in range(GRID_C):

        @pl.when(chan == 0)
        def _():
            rims[col * GRID_R] = beyond
            for part in range(2):
                table[col * GRID_R, part * RIM : (part + 1) * RIM] = beyond

        @pl.when(chan == CHAN - 1)
        def _():
            rims[(col + 1) * GRID_R - 1] = beyond
            for part in range(2):
                table[(col + 1) * GRID_R - 1, part * RIM : (part + 1) * RIM] = beyond

    def exchange(buffer, send, recv, kind, which):
        for at, (src, dst, many, ready, to, needed, _) in enumerate(moves):
            if ready[kind] == which:
                copy = remote(
                    buffer.at[pl.ds(src, many)], buffer.at[pl.ds(dst, many)], send.at[at], recv.at[at], to
                )
                when(needed, copy.start)

    def arrived(buffer, send, recv):
        for at, (src, dst, many, _, to, needed, coming) in enumerate(moves):
            copy = remote(
                buffer.at[pl.ds(src, many)], buffer.at[pl.ds(dst, many)], send.at[at], recv.at[at], to
            )
            when(coming, copy.wait_recv)

    def departed(buffer, send, recv):
        for at, (src, dst, many, _, to, needed, _) in enumerate(moves):
            copy = remote(
                buffer.at[pl.ds(src, many)], buffer.at[pl.ds(dst, many)], send.at[at], recv.at[at], to
            )
            when(needed, copy.wait_send)

    def pieces_in(col):
        for step in range(GROUP):
            source = lax.rem(rank + step, GROUP)
            far = place * COLS + col - source
            for c in range(CHAN):
                at = lax.rem(chan + c, CHAN)
                if step == 0 and c == 0:
                    when(stays[col][1], stays[col][0].wait)
                else:
                    arrival = remote(
                        payload.at[0, 0],
                        got[col].at[source, at],
                        spread_send.at[0],
                        spread_recv.at[(source * CHAN + at) * COLS + col],
                        (device, at),
                    )
                    when((far >= 0) & (far < HELD), arrival.wait_recv)

    row = lax.broadcasted_iota(jnp.int32, (RIM, CELLS), 0)
    cell = lax.broadcasted_iota(jnp.int32, (RIM, CELLS), 1)
    edge, along = row >> 3, row & 7
    at_rim = jnp.where(
        edge == 0, along, jnp.where(edge == 1, 56 + along, jnp.where(edge == 2, along * 8, along * 8 + 7))
    )
    at_rim = jnp.where(cell == at_rim, 1.0, 0.0).astype(BF16)
    gain_of = lambda gain: gain[...].reshape(1, D)
    wide_lane = lax.broadcasted_iota(jnp.int32, (48, 128), 1)
    masks = []
    wanted = []
    for col in range(COLS):
        pieces_in(col)
        blocks = [got[col][sources[col], c, PIECE - 1].astype(F32) for c in range(CHAN)]
        all_wanted = rim_wanted(blocks[0][0:8], blocks[0][8:16])
        for r in range(ROWS):
            slot = chan * ROWS + r
            wanted.append(
                jnp.sum(jnp.where(wide_lane == slot + FACE, all_wanted, 0.0), axis=1, keepdims=True)
            )
            pieces, column = [], []
            for c in range(CHAN):
                pieces.append(
                    jnp.concatenate([got[col][sources[col], c, r * 3 + part] for part in range(3)], axis=1)
                )
                column.append(jnp.sum(jnp.where(lane == slot, blocks[c], 0.0), axis=1, keepdims=True))
            values = jnp.concatenate(pieces, axis=0)
            mask = jnp.concatenate(column, axis=0)
            masks.append(mask)
            tile = col * ROWS + r
            own[tile * CELLS : (tile + 1) * CELLS] = values
            norm = (rms(values.astype(F32), gain_of(gain_image)) * mask).astype(BF16)
            normed[tile] = norm
            rims[(1 + col) * GRID_R + 1 + r] = jnp.dot(at_rim, norm, preferred_element_type=F32).astype(BF16)
        exchange(rims, rim_send, rim_recv, 0, col)
        for tile in range(col * ROWS, (col + 1) * ROWS):
            frame[tile, 1:9, 8:16, :] = normed[tile].astype(F32).reshape(SIDE, SIDE, D)

    loads[0].wait()
    arrived(rims, rim_send, rim_recv)

    rim_lane = lax.broadcasted_iota(jnp.int32, (48, SPOTS * RIM), 1).astype(F32)
    for part in range(0, ROWS, PART):
        for col in range(COLS):
            for r in range(part, part + PART):
                tile = col * ROWS + r
                at = part * COLS + col * PART + r - part
                chosen = jnp.where(rim_lane == wanted[tile], 1.0, 0.0).astype(BF16)
                rim = jnp.dot(chosen, rims[...].reshape(SPOTS * RIM, D), preferred_element_type=F32)
                frame[tile, 0, 8:16, :] = rim[0:8]
                frame[tile, 9, 8:16, :] = rim[8:16]
                for i in range(SIDE):
                    frame[tile, 1 + i, 7:8, :] = rim[16 + i : 17 + i]
                    frame[tile, 1 + i, 16:17, :] = rim[24 + i : 25 + i]
                frame[tile, 0, 7:8, :] = rim[32:33]
                frame[tile, 0, 16:17, :] = rim[33:34]
                frame[tile, 9, 7:8, :] = rim[34:35]
                frame[tile, 9, 16:17, :] = rim[35:36]
                for tap in range(9):
                    dr, dc = tap // 3, tap % 3
                    window = frame[tile, dr : dr + SIDE, 7 + dc : 7 + dc + SIDE, :]
                    patches[at * CELLS : (at + 1) * CELLS, tap * D : (tap + 1) * D] = window.reshape(
                        CELLS, D
                    ).astype(BF16)
        total = jnp.dot(
            patches[part * COLS * CELLS : (part + PART) * COLS * CELLS, :], conv[...], preferred_element_type=F32
        )
        for col in range(COLS):
            tile = col * ROWS + part
            rows = slice(tile * CELLS, (tile + PART) * CELLS)
            mine = total[col * PART * CELLS : (col + 1) * PART * CELLS]
            image = (own[rows, :].astype(F32) + mine).astype(BF16)
            after[rows, :] = image
            mask = jnp.concatenate(masks[tile : tile + PART], axis=0)
            attn = (rms(image.astype(F32), gain_of(gain_attn)) * mask).astype(BF16)
            spot = (1 + col) * GRID_R + 1 + part
            table[spot : spot + PART] = attn.reshape(PART, CELLS, D)
        exchange(table, halo_send, halo_recv, 1, part)

    def project(spot, many):
        rows = table[spot : spot + many].reshape(many * CELLS, D)
        found = jnp.dot(rows, qkv[:, D:], preferred_element_type=F32)
        memory[spot * CELLS : (spot + many) * CELLS, :] = found.astype(BF16)

    loads[1].wait()
    scale = 1.0 / math.sqrt(HEAD_DIM)
    for col in range(COLS):
        spot = (1 + col) * GRID_R + 1
        found = jnp.dot(
            table[spot : spot + ROWS].reshape(HALF, D), qkv[:, :D], preferred_element_type=F32
        )
        queries[col * HALF : (col + 1) * HALF, :] = (found * scale).astype(BF16)
        project(spot, ROWS)
    for load in loads[2:]:
        load.wait()
    arrived(table, halo_send, halo_recv)
    project(0, GRID_R + 1)
    project(GRID_R + ROWS + 1, 2)
    project(2 * GRID_R + ROWS + 1, GRID_R + 1)

    def heads_step(rows, first, lanes, base):
        heads = lanes // HEAD_DIM
        head = lax.broadcasted_iota(jnp.int32, (CELLS, lanes), 1) >> 6
        query = queries[rows, first : first + lanes]
        nothing = jnp.zeros_like(query)
        blocks = jnp.concatenate([jnp.where(head == h, query, nothing) for h in range(heads)], axis=0)
        spots = slice(base, base + 9 * CELLS)
        scores = lax.dot_general(
            blocks, keys[spots, first : first + lanes], (((1,), (1,)), ((), ())), preferred_element_type=F32
        )
        weights = jnp.exp(scores - jnp.max(scores, axis=-1, keepdims=True))
        total = jnp.sum(weights, axis=-1, keepdims=True)
        value = jnp.dot(
            weights.astype(BF16), keys[spots, D + first : D + first + lanes], preferred_element_type=F32
        )
        value = value / total
        found = value[:CELLS]
        for h in range(1, heads):
            found = jnp.where(head == h, value[h * CELLS : (h + 1) * CELLS], found)
        mixed[rows, first : first + lanes] = found.astype(BF16)

    returned = []
    for col in range(COLS):

        def attend(r):
            base_key = r % PART * 9 * CELLS
            for n in range(3):
                spot = (col + n) * GRID_R + r
                keys[base_key + n * 3 * CELLS : base_key + (n + 1) * 3 * CELLS, :] = memory[
                    spot * CELLS : (spot + 3) * CELLS, :
                ]
            rows = slice((col * ROWS + r) * CELLS, (col * ROWS + r + 1) * CELLS)
            heads_step(rows, 0, 4 * HEAD_DIM, base_key)
            heads_step(rows, 4 * HEAD_DIM, 2 * HEAD_DIM, base_key)

        for part in range(0, ROWS, PART):
            for r in range(part, part + PART):
                attend(r)
            rows = slice(col * HALF + part * CELLS, col * HALF + (part + PART) * CELLS)
            attended = jnp.dot(mixed[rows, :], proj[...], preferred_element_type=F32)
            attended = (after[rows, :].astype(F32) + attended).astype(BF16)
            wide = attended.astype(F32)
            hidden = jnp.dot(rms(wide, gain_of(gain_mlp)).astype(BF16), up[...], preferred_element_type=F32)
            hidden = (0.5 * hidden * (1.0 + lax.erf(hidden * (0.5**0.5)))).astype(BF16)
            encoded = wide + jnp.dot(hidden, down[...], preferred_element_type=F32)
            encoded = encoded.astype(BF16).reshape(PART, CHAN, 16, D)
            for r in range(PART):
                for c in range(CHAN):
                    tiles[col, c, part + r] = encoded[r, c]
            span = pl.ds(part, PART)
            for c in (2, 3, 1, 0):
                to = lax.rem(chan + c, CHAN)
                for step in range(GROUP):
                    target = lax.rem(rank + step, GROUP)
                    i = place * COLS + col - target
                    slot = limit(i, HELD - 1)
                    inside = (i >= 0) & (i < HELD)
                    if c == 0 and step == 0:
                        copy = pltpu.make_async_copy(
                            tiles.at[col, chan, span],
                            home.at[slot, chan, span],
                            local.at[COLS + (col * ROWS + part) // PART],
                        )
                    else:
                        copy = remote(
                            tiles.at[col, to, span],
                            home.at[slot, chan, span],
                            home_send.at[len(returned)],
                            home_recv.at[(slot * CHAN + chan) * (ROWS // PART) + part // PART],
                            (base + target, to),
                        )
                    when(inside, copy.start)
                    returned.append((copy, inside, c == 0 and step == 0))

    departed(rims, rim_send, rim_recv)
    departed(table, halo_send, halo_recv)
    for copy, needed in sent:
        when(needed, copy.wait_send)
    for copy, inside, stays_here in returned:
        when(inside, copy.wait if stays_here else copy.wait_send)
    for i in range(HELD):
        worker = snake((rank + i) // COLS)
        for c in range(CHAN):
            at = lax.rem(chan + c, CHAN)
            for part in range(0, ROWS, PART):
                span = pl.ds(part, PART)
                arrival = remote(
                    tiles.at[0, 0, span],
                    home.at[i, at, span],
                    home_send.at[0],
                    home_recv.at[(i * CHAN + at) * (ROWS // PART) + part // PART],
                    (device, at),
                )
                when(None if c else worker != rank, arrival.wait_recv)


def settle_kernel(where, home, out, columns, blank, come, go):
    shift, count = where[0], where[1]

    def fetch(i):
        return pltpu.make_async_copy(home.at[jnp.minimum(i + shift, HELD - 1)], columns.at[i], come.at[i])

    for i in range(HELD):
        pl.when(i < count)(fetch(i).start)
    blank[...] = jnp.zeros_like(blank)
    for i in range(HELD):

        @pl.when(i < count)
        def _():
            fetch(i).wait()
            pltpu.make_async_copy(columns.at[i], out.at[i], go.at[i]).start()

        @pl.when(i >= count)
        def _():
            pltpu.make_async_copy(blank, out.at[i], go.at[i]).start()

    for i in range(HELD):
        pltpu.make_async_copy(blank, out.at[i], go.at[i]).wait()


def per_device(
    latents,
    owner,
    neighbours,
    rotations,
    cell_mask,
    gain_image,
    conv_weight,
    gain_attn,
    qkv_weight,
    out_weight,
    gain_mlp,
    up_weight,
    down_weight,
):
    weights = [conv_weight, qkv_weight, out_weight, up_weight, down_weight]
    vmem = pltpu.VMEM
    dma = pltpu.SemaphoreType.DMA
    moves = 8 + 2 * COLS
    home, where = pl.pallas_call(
        block_kernel,
        out_shape=(
            jax.ShapeDtypeStruct((HELD, CHAN, ROWS, 16, D), BF16),
            jax.ShapeDtypeStruct((2,), jnp.int32),
        ),
        in_specs=[HBM] + [VMEM] * 3 + [HBM] + [VMEM] * 3 + [HBM] * 5,
        out_specs=(HBM, SMEM),
        scratch_shapes=[
            pltpu.SMEM((FACE * BAND,), jnp.int32),
            vmem((32, 128), jnp.int32),
            vmem((HELD, FACE, 16, D), BF16),
            vmem((HELD, CHAN, PIECE, 16, 128), BF16),
            vmem((GROUP, CHAN, PIECE, 16, 128), BF16),
            vmem((GROUP, CHAN, PIECE, 16, 128), BF16),
            vmem((OWN * CELLS, D), BF16),
            vmem((OWN, CELLS, D), BF16),
            vmem((HELD, FACE, 128), BF16),
            vmem((SPOTS, RIM, D), BF16),
            vmem((OWN, 10, 24, D), F32),
            vmem((OWN * CELLS, 9 * D), BF16),
            vmem((OWN * CELLS, D), BF16),
            vmem((SPOTS, CELLS, D), BF16),
            vmem((SPOTS * CELLS, 2 * D), BF16),
            vmem((OWN * CELLS, D), BF16),
            vmem((PART * 9 * CELLS, 2 * D), BF16),
            vmem((OWN * CELLS, D), BF16),
            vmem((COLS, CHAN, ROWS, 16, D), BF16),
            *[vmem(w.shape, BF16) for w in weights],
            dma((7,)),
            dma((HELD * CHAN,)),
            dma((GROUP * CHAN * COLS,)),
            dma((moves,)),
            dma((moves,)),
            dma((moves,)),
            dma((moves,)),
            dma((GROUP * CHAN * OWN // PART,)),
            dma((HELD * CHAN * ROWS // PART,)),
            dma((COLS + OWN // PART,)),
        ],
        compiler_params=pltpu.CompilerParams(
            collective_id=0, has_side_effects=True, vmem_limit_bytes=60 << 20
        ),
        name="encoder_block",
    )(
        owner,
        cell_mask.T,
        neighbours.T,
        rotations.T,
        latents.reshape(HELD, FACE, 16, D),
        gain_image,
        gain_attn,
        gain_mlp,
        *weights,
    )
    out = pl.pallas_call(
        settle_kernel,
        out_shape=jax.ShapeDtypeStruct((HELD, FACE, 16, D), BF16),
        in_specs=[SMEM, HBM],
        out_specs=HBM,
        scratch_shapes=[
            vmem((HELD, FACE, 16, D), BF16),
            vmem((FACE, 16, D), BF16),
            dma((HELD,)),
            dma((HELD,)),
        ],
        name="settle",
    )(where, home.reshape(HELD, FACE, 16, D))
    return out.reshape(SLOTS, 16, D)


def solution(mesh):
    in_specs = (
        P("tiles", "chan", None),
        P(),
        P("tiles", None),
        P("tiles", None),
        P("tiles", "chan"),
        P(),
        P(),
        P(),
        P(),
        P(),
        P(),
        P(),
        P(),
    )
    return jax.shard_map(
        per_device,
        mesh=mesh,
        in_specs=in_specs,
        out_specs=P("tiles", "chan", None),
        check_vma=False,
    )
```

time: 70.3 us -> 64.9 us (0.923)
  Pallas kernels: 67.6 us -> 64.3 us
  local copies, waits for them, and re-layouts: 2.24 us -> 0 us
    pallas_call x1 -> x2, Pallas kernels: 67.6 us -> 64.3 us  [the longest x1 61.7 us: per_device(): pl.pallas_call(block_kernel, out_shape=(jax.ShapeDtypeStruct((HELD, CHAN,...]
    unnamed x1 -> x0, local copies, waits for them, and re-layouts: 2.24 us -> none
where the time goes in v3:
time: 64.9 us; the launch traced here: 64.3 us
  Pallas kernels  64.3 us (99%)
    pallas_call x1, Pallas kernels, per_device(): pl.pallas_call(block_kernel, out_shape=(jax.ShapeDtypeStruct((HELD, CHAN,...  61.7 us
    pallas_call x1, Pallas kernels, per_device(): pl.pallas_call(settle_kernel, out_shape=jax.ShapeDtypeStruct((HELD, FACE,...  2.62 us

profile of v3, /device:TPU:1, one launch (start us, length us, event | category | flops | bytes accessed | tf_op | source)
XLA Modules:
  0.0 64.3 jit_solution(2830940231598148042)
XLA Ops:
  0.0 61.7 %encoder_block.1 = (bf16[5,4,4,16,384]{4,3,2,1,0:T(8,128)(2,1)}, s32[2]{0:T(128)}) custom-call(s32[1024]{0:T(1024)} %owner_hbm.1, s32[16,80]{1,0:T(8,128)} %bitcast.8, s32[8,80]{1,0:T(8,128)} %bitcast.9, s32[8,80]{1,0:T(8,128)} %bitcast.10, bf16[5,16,16,384]{3,2,1,0:T(8,128)(2,1)} %bitcast.6, f32[384]{0:T(512)} %gain_image.1, f32[384]{0:T(512)} %gain_attn.1, ...), custom_call_target="tpu_custom_call" | custom-call | tf_op jit(solution)/shard_map/encoder_block/pallas_call | solution.py:586
  61.7 2.6 %settle.1 = bf16[5,16,16,384]{3,2,1,0:T(8,128)(2,1)} custom-call(s32[2]{0:T(128)} %get-tuple-element.7.where, bf16[5,16,16,384]{3,2,1,0:T(8,128)(2,1)} %bitcast.7), custom_call_target="tpu_custom_call" | custom-call | tf_op jit(solution)/shard_map/settle/pallas_call | solution.py:641

commit v4 on v3

--- a/solution.py
+++ b/solution.py
@@ -9,7 +9,6 @@
 
 MESH = pl.DeviceIdType.MESH
 VMEM = pl.BlockSpec(memory_space=pltpu.VMEM)
-SMEM = pl.BlockSpec(memory_space=pltpu.SMEM)
 HBM = pl.BlockSpec(memory_space=pltpu.HBM)
 F32, BF16 = jnp.float32, jnp.bfloat16
 
@@ -135,21 +134,27 @@
 
 def block_kernel(
     owner_hbm,
-    mask_in,
-    near_in,
-    turn_in,
+    mask_hbm,
+    near_hbm,
+    turn_hbm,
     latents,
-    gain_image,
-    gain_attn,
-    gain_mlp,
+    image_hbm,
+    attn_hbm,
+    mlp_hbm,
     conv_hbm,
     qkv_hbm,
     proj_hbm,
     up_hbm,
     down_hbm,
+    out,
+    owner,
+    mask_in,
+    near_in,
+    turn_in,
+    gain_image,
+    gain_attn,
+    gain_mlp,
     home,
-    where,
-    owner,
     raw,
     held,
     payload,
@@ -193,6 +198,19 @@
     got = (got_first, got_second)
     owner_load = pltpu.make_async_copy(owner_hbm, owner, load_sem.at[6])
     owner_load.start()
+    small_loads = []
+    for at, (src, dst) in enumerate(
+        [
+            (mask_hbm, mask_in),
+            (near_hbm, near_in),
+            (turn_hbm, turn_in),
+            (image_hbm, gain_image),
+            (attn_hbm, gain_attn),
+            (mlp_hbm, gain_mlp),
+        ]
+    ):
+        small_loads.append(pltpu.make_async_copy(src, dst, load_sem.at[7 + at]))
+        small_loads[-1].start()
     first_load = pltpu.make_async_copy(latents, held, load_sem.at[0])
     first_load.start()
     loads = []
@@ -223,11 +241,12 @@
     start, count = lax.fori_loop(0, BAND, count_columns, (jnp.int32(0), jnp.int32(0)))
     limit = lambda value, top: jnp.minimum(jnp.maximum(value, 0), top)
     shift = limit(start - base * COLS - rank, HELD - 1)
-    where[0], where[1] = shift, count
     sources = [
         limit(owner[((base + place) * COLS + col) * FACE] - base, GROUP - 1) for col in range(COLS)
     ]
 
+    for load in small_loads:
+        load.wait()
     raw[...] = jnp.zeros_like(raw)
     raw[0:16, 0:SLOTS] = mask_in[...]
     raw[16:24, 0:SLOTS] = near_in[...]
@@ -358,12 +377,8 @@
     for col in range(COLS):
         pieces_in(col)
         blocks = [got[col][sources[col], c, PIECE - 1].astype(F32) for c in range(CHAN)]
-        all_wanted = rim_wanted(blocks[0][0:8], blocks[0][8:16])
         for r in range(ROWS):
             slot = chan * ROWS + r
-            wanted.append(
-                jnp.sum(jnp.where(wide_lane == slot + FACE, all_wanted, 0.0), axis=1, keepdims=True)
-            )
             pieces, column = [], []
             for c in range(CHAN):
                 pieces.append(
@@ -379,6 +394,10 @@
             normed[tile] = norm
             rims[(1 + col) * GRID_R + 1 + r] = jnp.dot(at_rim, norm, preferred_element_type=F32).astype(BF16)
         exchange(rims, rim_send, rim_recv, 0, col)
+        all_wanted = rim_wanted(blocks[0][0:8], blocks[0][8:16])
+        for r in range(ROWS):
+            slot = chan * ROWS + r + FACE
+            wanted.append(jnp.sum(jnp.where(wide_lane == slot, all_wanted, 0.0), axis=1, keepdims=True))
         for tile in range(col * ROWS, (col + 1) * ROWS):
             frame[tile, 1:9, 8:16, :] = normed[tile].astype(F32).reshape(SIDE, SIDE, D)
 
@@ -518,12 +537,6 @@
                     when(inside, copy.start)
                     returned.append((copy, inside, c == 0 and step == 0))
 
-    departed(rims, rim_send, rim_recv)
-    departed(table, halo_send, halo_recv)
-    for copy, needed in sent:
-        when(needed, copy.wait_send)
-    for copy, inside, stays_here in returned:
-        when(inside, copy.wait if stays_here else copy.wait_send)
     for i in range(HELD):
         worker = snake((rank + i) // COLS)
         for c in range(CHAN):
@@ -539,29 +552,18 @@
                 )
                 when(None if c else worker != rank, arrival.wait_recv)
 
-
-def settle_kernel(where, home, out, columns, blank, come, go):
-    shift, count = where[0], where[1]
-
-    def fetch(i):
-        return pltpu.make_async_copy(home.at[jnp.minimum(i + shift, HELD - 1)], columns.at[i], come.at[i])
-
+    departed(rims, rim_send, rim_recv)
+    departed(table, halo_send, halo_recv)
+    for copy, needed in sent:
+        when(needed, copy.wait_send)
+    for copy, inside, stays_here in returned:
+        when(inside, copy.wait if stays_here else copy.wait_send)
     for i in range(HELD):
-        pl.when(i < count)(fetch(i).start)
-    blank[...] = jnp.zeros_like(blank)
-    for i in range(HELD):
-
-        @pl.when(i < count)
-        def _():
-            fetch(i).wait()
-            pltpu.make_async_copy(columns.at[i], out.at[i], go.at[i]).start()
-
-        @pl.when(i >= count)
-        def _():
-            pltpu.make_async_copy(blank, out.at[i], go.at[i]).start()
-
-    for i in range(HELD):
-        pltpu.make_async_copy(blank, out.at[i], go.at[i]).wait()
+        column = limit(i + shift, HELD - 1)
+        for c in range(CHAN):
+            for r in range(ROWS):
+                values = home[column, c, r]
+                out[i, c * ROWS + r] = lax.select(i < count, values, jnp.zeros_like(values))
 
 
 def per_device(
@@ -583,16 +585,20 @@
     vmem = pltpu.VMEM
     dma = pltpu.SemaphoreType.DMA
     moves = 8 + 2 * COLS
-    home, where = pl.pallas_call(
+    out = pl.pallas_call(
         block_kernel,
-        out_shape=(
-            jax.ShapeDtypeStruct((HELD, CHAN, ROWS, 16, D), BF16),
-            jax.ShapeDtypeStruct((2,), jnp.int32),
-        ),
-        in_specs=[HBM] + [VMEM] * 3 + [HBM] + [VMEM] * 3 + [HBM] * 5,
-        out_specs=(HBM, SMEM),
+        out_shape=jax.ShapeDtypeStruct((HELD, FACE, 16, D), BF16),
+        in_specs=[HBM] * 13,
+        out_specs=VMEM,
         scratch_shapes=[
             pltpu.SMEM((FACE * BAND,), jnp.int32),
+            vmem((16, SLOTS), jnp.int32),
+            vmem((8, SLOTS), jnp.int32),
+            vmem((8, SLOTS), jnp.int32),
+            vmem((D,), F32),
+            vmem((D,), F32),
+            vmem((D,), F32),
+            vmem((HELD, CHAN, ROWS, 16, D), BF16),
             vmem((32, 128), jnp.int32),
             vmem((HELD, FACE, 16, D), BF16),
             vmem((HELD, CHAN, PIECE, 16, 128), BF16),
@@ -612,7 +618,7 @@
             vmem((OWN * CELLS, D), BF16),
             vmem((COLS, CHAN, ROWS, 16, D), BF16),
             *[vmem(w.shape, BF16) for w in weights],
-            dma((7,)),
+            dma((13,)),
             dma((HELD * CHAN,)),
             dma((GROUP * CHAN * COLS,)),
             dma((moves,)),
@@ -638,19 +644,6 @@
         gain_mlp,
         *weights,
     )
-    out = pl.pallas_call(
-        settle_kernel,
-        out_shape=jax.ShapeDtypeStruct((HELD, FACE, 16, D), BF16),
-        in_specs=[SMEM, HBM],
-        out_specs=HBM,
-        scratch_shapes=[
-            vmem((HELD, FACE, 16, D), BF16),
-            vmem((FACE, 16, D), BF16),
-            dma((HELD,)),
-            dma((HELD,)),
-        ],
-        name="settle",
-    )(where, home.reshape(HELD, FACE, 16, D))
     return out.reshape(SLOTS, 16, D)
 
 

time: 64.9 us -> 64.5 us (level)
  local copies, waits for them, and re-layouts: 0 us -> 2.24 us
  Pallas kernels: 64.3 us -> 62.1 us
    unnamed x0 -> x1, local copies, waits for them, and re-layouts: none -> 2.24 us
    pallas_call x2 -> x1, Pallas kernels: 64.3 us -> 62.1 us  [per_device(): pl.pallas_call(block_kernel, out_shape=jax.ShapeDtypeStruct((HELD, FACE,...]
where the time goes in v4:
time: 64.5 us; the launch traced here: 64.3 us
  Pallas kernels  62.1 us (96%)
  local copies, waits for them, and re-layouts  2.24 us (3%)
    pallas_call x1, Pallas kernels, per_device(): pl.pallas_call(block_kernel, out_shape=jax.ShapeDtypeStruct((HELD, FACE,...  62.1 us
    unnamed x1, local copies, waits for them, and re-layouts  2.24 us

profile of v4, /device:TPU:1, one launch (start us, length us, event | category | flops | bytes accessed | tf_op | source)
XLA Modules:
  0.0 64.3 jit_solution(1423330007638827562)
XLA Ops:
  0.0 62.1 %encoder_block.1 = bf16[5,16,16,384]{3,2,1,0:T(8,128)(2,1)} custom-call(s32[1024]{0:T(1024)} %owner_hbm.1, s32[16,80]{1,0:T(8,128)} %bitcast.7, s32[8,80]{1,0:T(8,128)} %bitcast.8, s32[8,80]{1,0:T(8,128)} %bitcast.9, bf16[5,16,16,384]{3,2,1,0:T(8,128)(2,1)} %bitcast.6, f32[384]{0:T(512)} %image_hbm.1, f32[384]{0:T(512)} %attn_hbm.1, f32[384]{0:T(512)} %mlp_hbm.1, ...), custom_call_target="tpu_custom_call" | custom-call | tf_op jit(solution)/shard_map/encoder_block/pallas_call | solution.py:588
  62.1 2.2 %copy.15 = bf16[80,16,384]{2,1,0:T(8,128)(2,1)} copy(bf16[80,16,384]{2,1,0:T(8,128)(2,1)} %bitcast.5) | data formatting | bytes 1966080

commit v5 on v4

--- a/solution.py
+++ b/solution.py
@@ -147,6 +147,7 @@
     up_hbm,
     down_hbm,
     out,
+    filled,
     owner,
     mask_in,
     near_in,
@@ -241,6 +242,7 @@
     start, count = lax.fori_loop(0, BAND, count_columns, (jnp.int32(0), jnp.int32(0)))
     limit = lambda value, top: jnp.minimum(jnp.maximum(value, 0), top)
     shift = limit(start - base * COLS - rank, HELD - 1)
+    filled[0] = count * FACE
     sources = [
         limit(owner[((base + place) * COLS + col) * FACE] - base, GROUP - 1) for col in range(COLS)
     ]
@@ -323,9 +325,9 @@
             for part in range(2):
                 table[(col + 1) * GRID_R - 1, part * RIM : (part + 1) * RIM] = beyond
 
-    def exchange(buffer, send, recv, kind, which):
+    def exchange(buffer, send, recv, cols, part):
         for at, (src, dst, many, ready, to, needed, _) in enumerate(moves):
-            if ready[kind] == which:
+            if ready[0] in cols and ready[1] == part:
                 copy = remote(
                     buffer.at[pl.ds(src, many)], buffer.at[pl.ds(dst, many)], send.at[at], recv.at[at], to
                 )
@@ -393,7 +395,8 @@
             norm = (rms(values.astype(F32), gain_of(gain_image)) * mask).astype(BF16)
             normed[tile] = norm
             rims[(1 + col) * GRID_R + 1 + r] = jnp.dot(at_rim, norm, preferred_element_type=F32).astype(BF16)
-        exchange(rims, rim_send, rim_recv, 0, col)
+            if r % PART == PART - 1:
+                exchange(rims, rim_send, rim_recv, (col,), r - PART + 1)
         all_wanted = rim_wanted(blocks[0][0:8], blocks[0][8:16])
         for r in range(ROWS):
             slot = chan * ROWS + r + FACE
@@ -440,7 +443,7 @@
             attn = (rms(image.astype(F32), gain_of(gain_attn)) * mask).astype(BF16)
             spot = (1 + col) * GRID_R + 1 + part
             table[spot : spot + PART] = attn.reshape(PART, CELLS, D)
-        exchange(table, halo_send, halo_recv, 1, part)
+        exchange(table, halo_send, halo_recv, (0, 1), part)
 
     def project(spot, many):
         rows = table[spot : spot + many].reshape(many * CELLS, D)
@@ -562,8 +565,7 @@
         column = limit(i + shift, HELD - 1)
         for c in range(CHAN):
             for r in range(ROWS):
-                values = home[column, c, r]
-                out[i, c * ROWS + r] = lax.select(i < count, values, jnp.zeros_like(values))
+                out[i, c * ROWS + r] = home[column, c, r]
 
 
 def per_device(
@@ -585,11 +587,14 @@
     vmem = pltpu.VMEM
     dma = pltpu.SemaphoreType.DMA
     moves = 8 + 2 * COLS
-    out = pl.pallas_call(
+    out, filled = pl.pallas_call(
         block_kernel,
-        out_shape=jax.ShapeDtypeStruct((HELD, FACE, 16, D), BF16),
+        out_shape=(
+            jax.ShapeDtypeStruct((HELD, FACE, 16, D), BF16),
+            jax.ShapeDtypeStruct((1,), jnp.int32),
+        ),
         in_specs=[HBM] * 13,
-        out_specs=VMEM,
+        out_specs=(VMEM, pl.BlockSpec(memory_space=pltpu.SMEM)),
         scratch_shapes=[
             pltpu.SMEM((FACE * BAND,), jnp.int32),
             vmem((16, SLOTS), jnp.int32),
@@ -644,7 +649,9 @@
         gain_mlp,
         *weights,
     )
-    return out.reshape(SLOTS, 16, D)
+    out = out.reshape(SLOTS, 16, D)
+    slot = lax.broadcasted_iota(jnp.int32, out.shape, 0)
+    return jnp.where(slot < filled[0], out, jnp.zeros_like(out))
 
 
 def solution(mesh):

time: 64.5 us -> 65.1 us (level)
  other arithmetic: 0 us -> 2.89 us
  local copies, waits for them, and re-layouts: 2.24 us -> 0 us
    select_n x0 -> x1, other arithmetic: none -> 2.33 us  [per_device(): return jnp.where(slot < filled[0], out, jnp.zeros_like(out))]
    unnamed x1 -> x0, local copies, waits for them, and re-layouts: 2.24 us -> none
where the time goes in v5:
time: 65.1 us; the launch traced here: 64.9 us
  Pallas kernels  62 us (95%)
  other arithmetic  2.89 us (4%)
    pallas_call x1, Pallas kernels, per_device(): pl.pallas_call(block_kernel, out_shape=(jax.ShapeDtypeStruct((HELD, FACE,...  62 us
    select_n x1, other arithmetic, per_device(): return jnp.where(slot < filled[0], out, jnp.zeros_like(out))  2.33 us

profile of v5, /device:TPU:1, one launch (start us, length us, event | category | flops | bytes accessed | tf_op | source)
XLA Modules:
  0.0 64.9 jit_solution(14074606818723146122)
XLA Ops:
  0.0 62.0 %encoder_block.1 = (bf16[5,16,16,384]{3,2,1,0:T(8,128)(2,1)}, s32[1]{0:T(128)}) custom-call(s32[1024]{0:T(1024)} %owner_hbm.1, s32[16,80]{1,0:T(8,128)} %bitcast.8, s32[8,80]{1,0:T(8,128)} %bitcast.9, s32[8,80]{1,0:T(8,128)} %bitcast.10, bf16[5,16,16,384]{3,2,1,0:T(8,128)(2,1)} %bitcast.7, f32[384]{0:T(512)} %image_hbm.1, f32[384]{0:T(512)} %attn_hbm.1, ...), custom_call_target="tpu_custom_call" | custom-call | tf_op jit(solution)/shard_map/encoder_block/pallas_call | solution.py:590
  62.0 0.6 iota_compare_fusion
  62.6 2.3 %bitcast_select_fusion = bf16[80,16,384]{2,1,0:T(8,128)(2,1)} fusion(bf16[5,16,16,384]{3,2,1,0:T(8,128)(2,1)} %get-tuple-element.8, pred[80]{0:T(512)(128)(4,1)S(1)} %iota_compare_fusion), kind=kLoop, calls=%fused_computation | loop fusion | flops 491520 | bytes 1966160 | tf_op jit(solution)/shard_map/jit(_where)/select_n | solution.py:654

commit v6 on v3

--- a/solution.py
+++ b/solution.py
@@ -387,12 +387,19 @@
 
     rim_lane = lax.broadcasted_iota(jnp.int32, (48, SPOTS * RIM), 1).astype(F32)
     for part in range(0, ROWS, PART):
+        chosen = [
+            jnp.where(rim_lane == wanted[col * ROWS + r], 1.0, 0.0).astype(BF16)
+            for col in range(COLS)
+            for r in range(part, part + PART)
+        ]
+        strips = jnp.dot(
+            jnp.concatenate(chosen, axis=0), rims[...].reshape(SPOTS * RIM, D), preferred_element_type=F32
+        )
         for col in range(COLS):
             for r in range(part, part + PART):
                 tile = col * ROWS + r
                 at = part * COLS + col * PART + r - part
-                chosen = jnp.where(rim_lane == wanted[tile], 1.0, 0.0).astype(BF16)
-                rim = jnp.dot(chosen, rims[...].reshape(SPOTS * RIM, D), preferred_element_type=F32)
+                rim = strips[(at - part * COLS) * 48 : (at - part * COLS + 1) * 48]
                 frame[tile, 0, 8:16, :] = rim[0:8]
                 frame[tile, 9, 8:16, :] = rim[8:16]
                 for i in range(SIDE):

time: 64.9 us -> 64.7 us (level)
  no operation moved by 1% of the time
where the time goes in v6:
time: 64.7 us; the launch traced here: 64.2 us
  Pallas kernels  64.2 us (99%)
    pallas_call x1, Pallas kernels, per_device(): pl.pallas_call(block_kernel, out_shape=(jax.ShapeDtypeStruct((HELD, CHAN,...  61.5 us
    pallas_call x1, Pallas kernels, per_device(): pl.pallas_call(settle_kernel, out_shape=jax.ShapeDtypeStruct((HELD, FACE,...  2.68 us

profile of v6, /device:TPU:1, one launch (start us, length us, event | category | flops | bytes accessed | tf_op | source)
XLA Modules:
  0.0 64.2 jit_solution(17184139619665273015)
XLA Ops:
  0.0 61.5 %encoder_block.1 = (bf16[5,4,4,16,384]{4,3,2,1,0:T(8,128)(2,1)}, s32[2]{0:T(128)}) custom-call(s32[1024]{0:T(1024)} %owner_hbm.1, s32[16,80]{1,0:T(8,128)} %bitcast.8, s32[8,80]{1,0:T(8,128)} %bitcast.9, s32[8,80]{1,0:T(8,128)} %bitcast.10, bf16[5,16,16,384]{3,2,1,0:T(8,128)(2,1)} %bitcast.6, f32[384]{0:T(512)} %gain_image.1, f32[384]{0:T(512)} %gain_attn.1, ...), custom_call_target="tpu_custom_call" | custom-call | tf_op jit(solution)/shard_map/encoder_block/pallas_call | solution.py:593
  61.6 2.7 %settle.1 = bf16[5,16,16,384]{3,2,1,0:T(8,128)(2,1)} custom-call(s32[2]{0:T(128)} %get-tuple-element.7.where, bf16[5,16,16,384]{3,2,1,0:T(8,128)(2,1)} %bitcast.7), custom_call_target="tpu_custom_call" | custom-call | tf_op jit(solution)/shard_map/settle/pallas_call | solution.py:648

commit v7 on v3

--- a/solution.py
+++ b/solution.py
@@ -312,12 +312,13 @@
                 )
                 when(needed, copy.start)
 
-    def arrived(buffer, send, recv):
+    def arrived(buffer, send, recv, first=0, end=SPOTS):
         for at, (src, dst, many, _, to, needed, coming) in enumerate(moves):
-            copy = remote(
-                buffer.at[pl.ds(src, many)], buffer.at[pl.ds(dst, many)], send.at[at], recv.at[at], to
-            )
-            when(coming, copy.wait_recv)
+            if first <= dst < end:
+                copy = remote(
+                    buffer.at[pl.ds(src, many)], buffer.at[pl.ds(dst, many)], send.at[at], recv.at[at], to
+                )
+                when(coming, copy.wait_recv)
 
     def departed(buffer, send, recv):
         for at, (src, dst, many, _, to, needed, _) in enumerate(moves):
@@ -423,10 +424,15 @@
             table[spot : spot + PART] = attn.reshape(PART, CELLS, D)
         exchange(table, halo_send, halo_recv, 1, part)
 
-    def project(spot, many):
-        rows = table[spot : spot + many].reshape(many * CELLS, D)
-        found = jnp.dot(rows, qkv[:, D:], preferred_element_type=F32)
-        memory[spot * CELLS : (spot + many) * CELLS, :] = found.astype(BF16)
+    def project(*spans):
+        rows = jnp.concatenate(
+            [table[spot : spot + many].reshape(many * CELLS, D) for spot, many in spans], axis=0
+        )
+        found = jnp.dot(rows, qkv[:, D:], preferred_element_type=F32).astype(BF16)
+        at = 0
+        for spot, many in spans:
+            memory[spot * CELLS : (spot + many) * CELLS, :] = found[at : at + many * CELLS]
+            at += many * CELLS
 
     loads[1].wait()
     scale = 1.0 / math.sqrt(HEAD_DIM)
@@ -436,13 +442,12 @@
             table[spot : spot + ROWS].reshape(HALF, D), qkv[:, :D], preferred_element_type=F32
         )
         queries[col * HALF : (col + 1) * HALF, :] = (found * scale).astype(BF16)
-        project(spot, ROWS)
+        project((spot, ROWS))
     for load in loads[2:]:
         load.wait()
-    arrived(table, halo_send, halo_recv)
-    project(0, GRID_R + 1)
-    project(GRID_R + ROWS + 1, 2)
-    project(2 * GRID_R + ROWS + 1, GRID_R + 1)
+    far = 3 * GRID_R
+    arrived(table, halo_send, halo_recv, 0, far)
+    project((0, GRID_R + 1), (GRID_R + ROWS + 1, 2), (2 * GRID_R + ROWS + 1, 1))
 
     def heads_step(rows, first, lanes, base):
         heads = lanes // HEAD_DIM
@@ -479,6 +484,9 @@
             heads_step(rows, 0, 4 * HEAD_DIM, base_key)
             heads_step(rows, 4 * HEAD_DIM, 2 * HEAD_DIM, base_key)
 
+        if col == 1:
+            arrived(table, halo_send, halo_recv, far, SPOTS)
+            project((far, GRID_R))
         for part in range(0, ROWS, PART):
             for r in range(part, part + PART):
                 attend(r)

time: 64.9 us -> 64.1 us (0.988)
  no operation moved by 1% of the time
where the time goes in v7:
time: 64.1 us; the launch traced here: 63.9 us
  Pallas kernels  63.9 us (100%)
    pallas_call x1, Pallas kernels, per_device(): pl.pallas_call(block_kernel, out_shape=(jax.ShapeDtypeStruct((HELD, CHAN,...  61.2 us
    pallas_call x1, Pallas kernels, per_device(): pl.pallas_call(settle_kernel, out_shape=jax.ShapeDtypeStruct((HELD, FACE,...  2.68 us

profile of v7, /device:TPU:1, one launch (start us, length us, event | category | flops | bytes accessed | tf_op | source)
XLA Modules:
  0.0 63.9 jit_solution(15367444732682789042)
XLA Ops:
  0.0 61.2 %encoder_block.1 = (bf16[5,4,4,16,384]{4,3,2,1,0:T(8,128)(2,1)}, s32[2]{0:T(128)}) custom-call(s32[1024]{0:T(1024)} %owner_hbm.1, s32[16,80]{1,0:T(8,128)} %bitcast.8, s32[8,80]{1,0:T(8,128)} %bitcast.9, s32[8,80]{1,0:T(8,128)} %bitcast.10, bf16[5,16,16,384]{3,2,1,0:T(8,128)(2,1)} %bitcast.6, f32[384]{0:T(512)} %gain_image.1, f32[384]{0:T(512)} %gain_attn.1, ...), custom_call_target="tpu_custom_call" | custom-call | tf_op jit(solution)/shard_map/encoder_block/pallas_call | solution.py:594
  61.2 2.7 %settle.1 = bf16[5,16,16,384]{3,2,1,0:T(8,128)(2,1)} custom-call(s32[2]{0:T(128)} %get-tuple-element.7.where, bf16[5,16,16,384]{3,2,1,0:T(8,128)(2,1)} %bitcast.7), custom_call_target="tpu_custom_call" | custom-call | tf_op jit(solution)/shard_map/settle/pallas_call | solution.py:649

commit v8 on v7

--- a/solution.py
+++ b/solution.py
@@ -123,6 +123,7 @@
         (second + 1, second + ROWS + 1, 1, (1, 0), (device, above), up, down),
         (second + ROWS, second, 1, (1, last), (device, below), down, up),
     ]
+    moves = moves[4:] + moves[:4]
     return moves, (left, right, above, below)
 
 

time: 64.1 us -> 64.5 us (level)
  no operation moved by 1% of the time
where the time goes in v8:
time: 64.5 us; the launch traced here: 64.3 us
  Pallas kernels  64.3 us (100%)
    pallas_call x1, Pallas kernels, per_device(): pl.pallas_call(block_kernel, out_shape=(jax.ShapeDtypeStruct((HELD, CHAN,...  61.6 us
    pallas_call x1, Pallas kernels, per_device(): pl.pallas_call(settle_kernel, out_shape=jax.ShapeDtypeStruct((HELD, FACE,...  2.65 us

profile of v8, /device:TPU:1, one launch (start us, length us, event | category | flops | bytes accessed | tf_op | source)
XLA Modules:
  0.0 64.3 jit_solution(6404621062949100780)
XLA Ops:
  0.0 61.6 %encoder_block.1 = (bf16[5,4,4,16,384]{4,3,2,1,0:T(8,128)(2,1)}, s32[2]{0:T(128)}) custom-call(s32[1024]{0:T(1024)} %owner_hbm.1, s32[16,80]{1,0:T(8,128)} %bitcast.8, s32[8,80]{1,0:T(8,128)} %bitcast.9, s32[8,80]{1,0:T(8,128)} %bitcast.10, bf16[5,16,16,384]{3,2,1,0:T(8,128)(2,1)} %bitcast.6, f32[384]{0:T(512)} %gain_image.1, f32[384]{0:T(512)} %gain_attn.1, ...), custom_call_target="tpu_custom_call" | custom-call | tf_op jit(solution)/shard_map/encoder_block/pallas_call | solution.py:595
  61.6 2.6 %settle.1 = bf16[5,16,16,384]{3,2,1,0:T(8,128)(2,1)} custom-call(s32[2]{0:T(128)} %get-tuple-element.7.where, bf16[5,16,16,384]{3,2,1,0:T(8,128)(2,1)} %bitcast.7), custom_call_target="tpu_custom_call" | custom-call | tf_op jit(solution)/shard_map/settle/pallas_call | solution.py:650
